TPU v7x, 32 devices: a whole 2x2x4 slice. The times are simulated.
32 devices in a mesh: task: 8 (over y, x, core), samp: 4 (over z).
Axes of the slice: x: 2, y: 2, z: 4, core: 2. Of those that a mesh axis runs over, the one named last changes fastest.
Arguments:
- cells: bfloat16 [8, 512, 4, 512], P('task', 'samp'), may hold values from -6 to 6
- out_grad: bfloat16 [8, 512, 4, 512], P('task', 'samp'), may hold values from -6 to 6
- sample_counts: int32 [8], P('task'), may hold values from 51 to 512, as said below
- feature_counts: int32 [8], P('task'), may hold values from 2 to 4, as said below
- sample_block: float32 [1049088], P(('task', 'samp'))
- sample_first: float32 [1049088], P(('task', 'samp'))
- sample_second: float32 [1049088], P(('task', 'samp')), as said below
- feature_block: float32 [1049088], P(('task', 'samp'))
- feature_first: float32 [1049088], P(('task', 'samp'))
- feature_second: float32 [1049088], P(('task', 'samp')), as said below
- mlp_block: float32 [2097664], P(('task', 'samp'))
- mlp_first: float32 [2097664], P(('task', 'samp'))
- mlp_second: float32 [2097664], P(('task', 'samp')), as said below
Outputs:
- layer_out: bfloat16 [8, 512, 4, 512], P('task', 'samp')
- cells_grad: float32 [8, 512, 4, 512], P('task', 'samp')
- sample_grad: float32 [1049088], P(('task', 'samp'))
- sample_first_new: float32 [1049088], P(('task', 'samp'))
- sample_second_new: float32 [1049088], P(('task', 'samp'))
- sample_master_new: float32 [1049088], P(('task', 'samp'))
- sample_weights_new: bfloat16 [1049088], P(('task', 'samp'))
- feature_grad: float32 [1049088], P(('task', 'samp'))
- feature_first_new: float32 [1049088], P(('task', 'samp'))
- feature_second_new: float32 [1049088], P(('task', 'samp'))
- feature_master_new: float32 [1049088], P(('task', 'samp'))
- feature_weights_new: bfloat16 [1049088], P(('task', 'samp'))
- mlp_grad: float32 [2097664], P(('task', 'samp'))
- mlp_first_new: float32 [2097664], P(('task', 'samp'))
- mlp_second_new: float32 [2097664], P(('task', 'samp'))
- mlp_master_new: float32 [2097664], P(('task', 'samp'))
- mlp_weights_new: bfloat16 [2097664], P(('task', 'samp'))
- norm_pairs: float32 [9, 2], replicated
Inputs may be any that keep to these rules, and one draw needn't show every extreme that they name: `sample_counts`: samples at or beyond a task's count are padding; some task fills all 512 slots. `feature_counts`: features at or beyond a task's count are padding; some task fills all 4 slots. `sample_second`: every entry is positive. `feature_second`: every entry is positive. `mlp_second`: every entry is positive.
All inputs are finite; a program needn't handle non-finite values.
Results may differ from a plain program's by a relative error of at most 0.025.
The roundings to bfloat16 on the way count: a program that leaves them out, or rounds other values in their place, can miss the bound.
Values may be sent and summed in bfloat16 or wider, within the bound.
A program may use at most 128 MiB of HBM per device.

v0:
```python
import jax
import jax.numpy as jnp
from jax import lax
from jax.sharding import PartitionSpec as P

D = 512
HEADS = 8
HEAD_DIM = 64
FF = 2048


EPS_NORM = 1e-05
EPS_ADAM = 1e-06
STEP_RATE = 0.5
BIG_NEGATIVE = -1e30


def normalize(hidden, gain_row):
    centre = jnp.mean(hidden, -1, keepdims=True)
    shifted = hidden - centre
    spread = jnp.mean(shifted * shifted, -1, keepdims=True)
    return shifted * lax.rsqrt(spread + EPS_NORM) * gain_row


def norm_backward(hidden, gain_row, normed_grad):
    _, pullback = jax.vjp(normalize, hidden, gain_row)
    return pullback(normed_grad)


def gelu_exact(upward):
    return jax.nn.gelu(upward, approximate=False)


def contract_rows(left, right):
    return lax.dot_general(
        left, right, (((0,), (0,)), ((), ())), preferred_element_type=jnp.float32
    )


def times_transpose(left, right):
    return lax.dot_general(
        left, right, (((1,), (1,)), ((), ())), preferred_element_type=jnp.float32
    )


def unpack(flat_params, width_in, width_mid):
    gain_row = flat_params[:D].astype(jnp.float32)
    w_in = flat_params[D : D + D * width_in].reshape(D, width_in)
    w_out = flat_params[D + D * width_in :].reshape(width_mid, D)
    return (gain_row, w_in, w_out)


def fetch_forward(master):
    return lax.all_gather(master.astype(jnp.bfloat16), ("task", "samp"), axis=0, tiled=True)


def fetch_again(master):
    return lax.all_gather(master.astype(jnp.bfloat16), ("task", "samp"), axis=0, tiled=True)


def reduce_grads(gain_grad, in_grad, out_grad_matrix):
    flat_grads = jnp.concatenate([gain_grad, in_grad.reshape(-1), out_grad_matrix.reshape(-1)])
    return lax.psum_scatter(flat_grads, ("task", "samp"), scatter_dimension=0, tiled=True)


def group_size(feature_total, most):
    chosen = 1
    for candidate in range(1, most + 1):
        if feature_total % candidate == 0:
            chosen = candidate
    return chosen


def lamb_prepare(grad_shard, master, first, second, width_in):
    first_new = 0.5 * first + 0.5 * grad_shard
    second_new = 0.5 * second + 0.5 * grad_shard * grad_shard
    direction = first_new / (jnp.sqrt(second_new) + EPS_ADAM)
    entries = master.shape[0]
    position = lax.axis_index(("task", "samp")) * entries + jnp.arange(entries, dtype=jnp.int32)
    segment = (position >= D).astype(jnp.int32) + (position >= D + D * width_in).astype(jnp.int32)
    member = segment[None, :] == jnp.arange(3, dtype=jnp.int32)[:, None]
    weight_sums = jnp.sum(jnp.where(member, (master * master)[None, :], 0.0), 1)
    update_sums = jnp.sum(jnp.where(member, (direction * direction)[None, :], 0.0), 1)
    return (first_new, second_new, direction, member, jnp.stack([weight_sums, update_sums], 1))


def lamb_finish(master, block_state, trust_ratio):
    factor = jnp.sum(jnp.where(block_state[3], trust_ratio[:, None], 0.0), 0)
    return master - STEP_RATE * factor * block_state[2]


def sample_scores(query_part, key_part, key_live, score_scale):
    scores = (
        jnp.einsum("qfhe,kfhe->fhqk", query_part, key_part, preferred_element_type=jnp.float32)
        * score_scale
    )
    return jnp.where(key_live, scores, BIG_NEGATIVE)


def sample_forward(queries, pairs_all, key_live, block_features, score_scale):
    local_rows, features = (queries.shape[0], queries.shape[1])

    def one_block(block_index, results):
        attended, log_totals = results
        offset = block_index * block_features
        query_part = lax.dynamic_slice_in_dim(queries, offset, block_features, 1)
        pair_part = lax.dynamic_slice_in_dim(pairs_all, offset, block_features, 1)
        scores = sample_scores(query_part, pair_part[:, :, 0], key_live, score_scale)
        row_top = jnp.max(scores, -1, keepdims=True)
        exponent = jnp.exp(scores - row_top)
        row_total = jnp.sum(exponent, -1, keepdims=True)
        probability = (exponent / row_total).astype(jnp.bfloat16)
        block_out = jnp.einsum(
            "fhqk,kfhe->qfhe", probability, pair_part[:, :, 1], preferred_element_type=jnp.float32
        )
        attended = lax.dynamic_update_slice_in_dim(
            attended, block_out.astype(jnp.bfloat16), offset, 1
        )
        log_totals = lax.dynamic_update_slice_in_dim(
            log_totals, (row_top + jnp.log(row_total))[..., 0], offset, 0
        )
        return (attended, log_totals)

    start_state = (
        jnp.zeros(queries.shape, jnp.bfloat16),
        jnp.zeros((features, HEADS, local_rows), jnp.float32),
    )
    return lax.fori_loop(0, features // block_features, one_block, start_state)


def query_side(query_part, pair_part, grad_part, log_part, key_live, score_scale):
    key_part = pair_part[:, :, 0]
    value_part = pair_part[:, :, 1]
    scores = sample_scores(query_part, key_part, key_live, score_scale)
    probability = jnp.exp(scores - log_part[..., None])
    prob_grad = jnp.einsum(
        "qfhe,kfhe->fhqk", grad_part, value_part, preferred_element_type=jnp.float32
    )
    row_inner = jnp.sum(probability * prob_grad, -1, keepdims=True)
    score_grad = (probability * (prob_grad - row_inner)).astype(jnp.bfloat16)
    query_block = (
        jnp.einsum("fhqk,kfhe->qfhe", score_grad, key_part, preferred_element_type=jnp.float32)
        * score_scale
    )
    return (probability, score_grad, row_inner, query_block)


def sample_backward(
    queries, pairs_all, key_live, log_totals, attended_grad, block_features, score_scale
):
    local_rows, features = (queries.shape[0], queries.shape[1])

    def one_block(block_index, results):
        query_grads, pair_grads = results
        offset = block_index * block_features
        query_part = lax.dynamic_slice_in_dim(queries, offset, block_features, 1)
        pair_part = lax.dynamic_slice_in_dim(pairs_all, offset, block_features, 1)
        grad_part = lax.dynamic_slice_in_dim(attended_grad, offset, block_features, 1)
        log_part = lax.dynamic_slice_in_dim(log_totals, offset, block_features, 0)
        probability, score_grad, row_inner, query_block = query_side(
            query_part, pair_part, grad_part, log_part, key_live, score_scale
        )
        key_block = (
            jnp.einsum(
                "fhqk,qfhe->kfhe", score_grad, query_part, preferred_element_type=jnp.float32
            )
            * score_scale
        )
        value_block = jnp.einsum(
            "fhqk,qfhe->kfhe",
            probability.astype(jnp.bfloat16),
            grad_part,
            preferred_element_type=jnp.float32,
        )
        pair_terms = jnp.stack([key_block, value_block], 2)
        pair_local = lax.psum_scatter(
            pair_terms.astype(jnp.bfloat16), "samp", scatter_dimension=0, tiled=True
        ).astype(jnp.float32)
        query_grads = lax.dynamic_update_slice_in_dim(query_grads, query_block, offset, 1)
        pair_grads = lax.dynamic_update_slice_in_dim(pair_grads, pair_local, offset, 1)
        return (query_grads, pair_grads)

    start_state = (
        jnp.zeros((local_rows, features, HEADS, HEAD_DIM), jnp.float32),
        jnp.zeros((local_rows, features, 2, HEADS, HEAD_DIM), jnp.float32),
    )
    return lax.fori_loop(0, features // block_features, one_block, start_state)


def on_device(
    cells,
    out_grad,
    sample_counts,
    feature_counts,
    sample_block,
    sample_first,
    sample_second,
    feature_block,
    feature_first,
    feature_second,
    mlp_block,
    mlp_first,
    mlp_second,
):
    local_rows, features = (cells.shape[1], cells.shape[2])
    flat_rows = local_rows * features
    seq_all = local_rows * lax.axis_size("samp")
    score_scale = HEAD_DIM ** (-0.5)
    block_features = group_size(features, max(1, 2048 // (HEADS * local_rows)))
    sample_index = lax.axis_index("samp") * local_rows + jnp.arange(local_rows, dtype=jnp.int32)
    sample_live = sample_index < sample_counts[0]
    key_live = jnp.arange(seq_all, dtype=jnp.int32) < sample_counts[0]
    feature_live = jnp.arange(features, dtype=jnp.int32) < feature_counts[0]
    cell_live = sample_live[:, None, None] & feature_live[None, :, None]
    hidden_in = cells[0].astype(jnp.float32)
    gain_one, in_one, out_one = unpack(fetch_forward(sample_block), 3 * D, D)
    normed_one = normalize(hidden_in, gain_one).astype(jnp.bfloat16)
    packed_one = jnp.dot(
        normed_one.reshape(flat_rows, D), in_one, preferred_element_type=jnp.float32
    )
    packed_one = packed_one.astype(jnp.bfloat16).reshape(local_rows, features, 3, HEADS, HEAD_DIM)
    queries_one = packed_one[:, :, 0]
    pairs_local = packed_one[:, :, 1:]
    pairs_all = lax.all_gather(pairs_local, "samp", axis=0, tiled=True)
    attended_one, log_totals = sample_forward(
        queries_one, pairs_all, key_live, block_features, score_scale
    )
    attended_one_rows = attended_one.reshape(flat_rows, D)
    branch_one = jnp.dot(attended_one_rows, out_one, preferred_element_type=jnp.float32)
    hidden_one = hidden_in + branch_one.reshape(local_rows, features, D)
    gain_two, in_two, out_two = unpack(fetch_forward(feature_block), 3 * D, D)
    normed_two = normalize(hidden_one, gain_two).astype(jnp.bfloat16).reshape(flat_rows, D)
    packed_two = jnp.dot(normed_two, in_two, preferred_element_type=jnp.float32)
    packed_two = packed_two.astype(jnp.bfloat16).reshape(local_rows, features, 3, HEADS, HEAD_DIM)
    queries_two, key_two, value_two = (
        packed_two[:, :, 0],
        packed_two[:, :, 1],
        packed_two[:, :, 2],
    )
    scores_two = (
        jnp.einsum("sqhe,skhe->shqk", queries_two, key_two, preferred_element_type=jnp.float32)
        * score_scale
    )
    scores_two = jnp.where(feature_live, scores_two, BIG_NEGATIVE)
    row_top = jnp.max(scores_two, -1, keepdims=True)
    exponent = jnp.exp(scores_two - row_top)
    probability_two = exponent / jnp.sum(exponent, -1, keepdims=True)
    prob_low_two = probability_two.astype(jnp.bfloat16)
    attended_two = jnp.einsum(
        "shqk,skhe->sqhe", prob_low_two, value_two, preferred_element_type=jnp.float32
    )
    attended_two_rows = attended_two.reshape(flat_rows, D).astype(jnp.bfloat16)
    branch_two = jnp.dot(attended_two_rows, out_two, preferred_element_type=jnp.float32)
    hidden_two = hidden_one + branch_two.reshape(local_rows, features, D)
    gain_three, up_weight, down_weight = unpack(fetch_forward(mlp_block), FF, FF)
    normed_three = normalize(hidden_two, gain_three).astype(jnp.bfloat16).reshape(flat_rows, D)
    upward = jnp.dot(normed_three, up_weight, preferred_element_type=jnp.float32)
    activated = gelu_exact(upward).astype(jnp.bfloat16)
    branch_three = jnp.dot(activated, down_weight, preferred_element_type=jnp.float32)
    hidden_three = hidden_two + branch_three.reshape(local_rows, features, D)
    layer_out = jnp.where(cell_live, hidden_three, 0.0).astype(jnp.bfloat16)[None]
    top_grad = jnp.where(cell_live, out_grad[0], jnp.zeros((), jnp.bfloat16))
    top_rows = top_grad.reshape(flat_rows, D)
    gain_three, up_weight, down_weight = unpack(fetch_again(mlp_block), FF, FF)
    down_grad = contract_rows(activated, top_rows)
    act_grad = times_transpose(top_rows, down_weight).astype(jnp.bfloat16)
    _, gelu_pull = jax.vjp(gelu_exact, upward)
    up_grad = gelu_pull(act_grad.astype(jnp.float32))[0].astype(jnp.bfloat16)
    upw_grad = contract_rows(normed_three, up_grad)
    normed_grad = times_transpose(up_grad, up_weight).reshape(local_rows, features, D)
    hidden_grad, gain_three_grad = norm_backward(hidden_two, gain_three, normed_grad)
    grad_two = top_grad.astype(jnp.float32) + hidden_grad
    mlp_shard = reduce_grads(gain_three_grad, upw_grad, down_grad)
    mlp_state = lamb_prepare(mlp_shard, mlp_block, mlp_first, mlp_second, FF)
    gain_two, in_two, out_two = unpack(fetch_again(feature_block), 3 * D, D)
    branch_grad = grad_two.astype(jnp.bfloat16).reshape(flat_rows, D)
    out_two_grad = contract_rows(attended_two_rows, branch_grad)
    attended_grad = (
        times_transpose(branch_grad, out_two)
        .astype(jnp.bfloat16)
        .reshape(local_rows, features, HEADS, HEAD_DIM)
    )
    prob_grad = jnp.einsum(
        "sqhe,skhe->shqk", attended_grad, value_two, preferred_element_type=jnp.float32
    )
    row_inner = jnp.sum(probability_two * prob_grad, -1, keepdims=True)
    score_grad = (probability_two * (prob_grad - row_inner)).astype(jnp.bfloat16)
    query_grad = (
        jnp.einsum("shqk,skhe->sqhe", score_grad, key_two, preferred_element_type=jnp.float32)
        * score_scale
    )
    key_grad = (
        jnp.einsum("shqk,sqhe->skhe", score_grad, queries_two, preferred_element_type=jnp.float32)
        * score_scale
    )
    value_grad = jnp.einsum(
        "shqk,sqhe->skhe", prob_low_two, attended_grad, preferred_element_type=jnp.float32
    )
    packed_grad = (
        jnp.stack([query_grad, key_grad, value_grad], 2)
        .astype(jnp.bfloat16)
        .reshape(flat_rows, 3 * D)
    )
    in_two_grad = contract_rows(normed_two, packed_grad)
    normed_grad = times_transpose(packed_grad, in_two).reshape(local_rows, features, D)
    hidden_grad, gain_two_grad = norm_backward(hidden_one, gain_two, normed_grad)
    grad_one = grad_two + hidden_grad
    feature_shard = reduce_grads(gain_two_grad, in_two_grad, out_two_grad)
    feature_state = lamb_prepare(feature_shard, feature_block, feature_first, feature_second, 3 * D)
    gain_one, in_one, out_one = unpack(fetch_again(sample_block), 3 * D, D)
    pairs_all = lax.all_gather(pairs_local, "samp", axis=0, tiled=True)
    branch_grad = grad_one.astype(jnp.bfloat16).reshape(flat_rows, D)
    out_one_grad = contract_rows(attended_one_rows, branch_grad)
    attended_grad = (
        times_transpose(branch_grad, out_one)
        .astype(jnp.bfloat16)
        .reshape(local_rows, features, HEADS, HEAD_DIM)
    )
    query_grads, pair_grads = sample_backward(
        queries_one, pairs_all, key_live, log_totals, attended_grad, block_features, score_scale
    )
    packed_grad = (
        jnp.concatenate([query_grads[:, :, None], pair_grads], 2)
        .astype(jnp.bfloat16)
        .reshape(flat_rows, 3 * D)
    )
    in_one_grad = contract_rows(normed_one.reshape(flat_rows, D), packed_grad)
    normed_grad = times_transpose(packed_grad, in_one).reshape(local_rows, features, D)
    hidden_grad, gain_one_grad = norm_backward(hidden_in, gain_one, normed_grad)
    cells_grad = (grad_one + hidden_grad)[None]
    sample_shard = reduce_grads(gain_one_grad, in_one_grad, out_one_grad)
    sample_state = lamb_prepare(sample_shard, sample_block, sample_first, sample_second, 3 * D)
    totals = lax.psum(
        jnp.concatenate([sample_state[4], feature_state[4], mlp_state[4]], 0), ("task", "samp")
    )
    norm_pairs = jnp.sqrt(totals)
    trust_ratio = norm_pairs[:, 0] / (norm_pairs[:, 1] + EPS_ADAM)
    sample_master = lamb_finish(sample_block, sample_state, trust_ratio[0:3])
    feature_master = lamb_finish(feature_block, feature_state, trust_ratio[3:6])
    mlp_master = lamb_finish(mlp_block, mlp_state, trust_ratio[6:9])
    return (
        layer_out,
        cells_grad,
        sample_shard,
        sample_state[0],
        sample_state[1],
        sample_master,
        sample_master.astype(jnp.bfloat16),
        feature_shard,
        feature_state[0],
        feature_state[1],
        feature_master,
        feature_master.astype(jnp.bfloat16),
        mlp_shard,
        mlp_state[0],
        mlp_state[1],
        mlp_master,
        mlp_master.astype(jnp.bfloat16),
        norm_pairs,
    )


def solution(mesh):
    placed = (
        P("task", "samp", None, None),
        P("task", "samp", None, None),
        P("task"),
        P("task"),
        P(("task", "samp")),
        P(("task", "samp")),
        P(("task", "samp")),
        P(("task", "samp")),
        P(("task", "samp")),
        P(("task", "samp")),
        P(("task", "samp")),
        P(("task", "samp")),
        P(("task", "samp")),
    )
    return jax.shard_map(
        on_device,
        mesh=mesh,
        in_specs=placed,
        out_specs=(
            P("task", "samp", None, None),
            P("task", "samp", None, None),
            P(("task", "samp")),
            P(("task", "samp")),
            P(("task", "samp")),
            P(("task", "samp")),
            P(("task", "samp")),
            P(("task", "samp")),
            P(("task", "samp")),
            P(("task", "samp")),
            P(("task", "samp")),
            P(("task", "samp")),
            P(("task", "samp")),
            P(("task", "samp")),
            P(("task", "samp")),
            P(("task", "samp")),
            P(("task", "samp")),
            P(),
        ),
        check_vma=False,
    )
```

profile of v0, /device:TPU:0, one launch (start us, length us, event | category | flops | bytes accessed | tf_op | source)
XLA Modules:
  0.0 993.6 jit_solution(12310253008946214869)
XLA Ops:
  25.1 180.7 %all-reduce.13.cloned.1.call-done = (bf16[1049088]{0:T(1024)(128)(2,1)}, bf16[1049088]{0:T(1024)(128)(2,1)}, bf16[2097664]{0:T(1024)(128)(2,1)}) async-done(((bf16[1049088]{0:T(1024)(128)(2,1)}, bf16[1049088]{0:T(1024)(128)(2,1)}, bf16[2097664]{0:T(1024)(128)(2,1)}), (bf16[1049088]{0:T(1024)(128)(2,1)}, bf16[1049088]{0:T(1024)(128)(2,1)}, bf16[2097664]{0:T(1024)(128)(2,1)})) %all-reduce.13.cloned.1.call-update) | async-done | bytes 8391696
  215.6 5.0 reshape.398
  228.0 5.3 fusion.123
  268.0 40.5 %all-gather.2.cloned.1.call-done = bf16[512,4,2,8,64]{0,4,3,2,1:T(8,128)(2,1)} async-done(((bf16[128,4,2,8,64]{0,4,3,2,1:T(8,128)(2,1)}), bf16[512,4,2,8,64]{0,4,3,2,1:T(8,128)(2,1)}) %all-gather.2.cloned.1.call-update) | async-done | bytes 4194320 | tf_op jit(solution)/shard_map/all_gather | solution.py:224
  313.2 20.1 %while.32 = (s32[]{:T(128)}, bf16[128,4,8,64]{0,3,2,1:T(8,128)(2,1)S(1)}, f32[4,8,128]{2,1,0:T(8,128)S(1)}, bf16[512,4,2,8,64]{0,4,3,1,2:T(8,128)(2,1)}, bf16[12...) while((s32[]{:T(128)}, ...), condition=%wide.region_5.6_spmd.clone, body=%wide.region_2.5_spmd.clone.sunk | while | flops 281147904 | bytes 32051924 | solution.py:128
  338.7 5.1 reshape.401
  347.3 6.3 fusion.129
  362.3 12.4 %multiply_convert_fusion.2 = (bf16[512,2048]{1,0:T(8,128)(2,1)}, f32[512,2048]{1,0:T(8,128)S(1)}, f32[512,2048]{1,0:T(8,128)S(1)}) fusion(bf16[512,512]{1,0:T(8,128)(2,1)} %reshape.402, bf16[512,2048]{1,0:T(8,128)(2,1)} %reshape.403), kind=kOutput, calls=%fused_computation.71 | convolution fusion | flops 1141899264 | bytes 13107200 | tf_op jit(solution)/shard_map/dot_general | solution.py:257
  382.6 5.1 multiply_reduce_fusion.2
  408.8 5.1 convolution_bitcast_fusion.1
  419.2 6.0 copy.142
  438.7 141.8 %while.33 = (s32[]{:T(128)}, bf16[128,4,8,64]{0,3,2,1:T(8,128)(2,1)}, bf16[128,4,2,8,64]{0,4,3,2,1:T(8,128)(2,1)}, bf16[512,4,2,8,64]{0,4,3,1,2:T(8,128)(2,1)}, ...) while((s32[]{:T(128)}, ...), condition=%wide.region_20.21_spmd.clone, body=%wide.region_17.20_spmd.clone.sunk | while | flops 689568256 | bytes 61929200 | solution.py:187
  448.8 7.4 copy.253
  456.2 6.8 reshape.437
  465.8 39.4 %reduce-scatter.6.cloned.1.call-done = bf16[128,2048]{1,0:T(8,128)(2,1)} async-done(((bf16[512,2048]{1,0:T(8,128)(2,1)}), bf16[128,2048]{1,0:T(8,128)(2,1)}) %reduce-scatter.6.cloned.1.call-update) | async-done | bytes 524304 | tf_op jit(solution)/shard_map/while
  518.9 7.4 copy.253
  526.4 6.8 reshape.437
  535.9 40.6 %reduce-scatter.6.cloned.1.call-done = bf16[128,2048]{1,0:T(8,128)(2,1)} async-done(((bf16[512,2048]{1,0:T(8,128)(2,1)}), bf16[128,2048]{1,0:T(8,128)(2,1)}) %reduce-scatter.6.cloned.1.call-update) | async-done | bytes 524304 | tf_op jit(solution)/shard_map/while
  582.1 5.2 copy.150
  632.6 5.4 pad_maximum_fusion.2
  638.1 8.6 pad_maximum_fusion.1
  659.5 4.9 fusion.81
  666.0 266.7 %all-reduce.11.cloned.1.call-done = (f32[1049088]{0:T(1024)}, f32[2097664]{0:T(1024)}, f32[1049088]{0:T(1024)}) async-done(((f32[1049088]{0:T(1024)}, f32[2097664]{0:T(1024)}, f32[1049088]{0:T(1024)}), (f32[1049088]{0:T(1024)}, f32[2097664]{0:T(1024)}, f32[1049088]{0:T(1024)})) %all-reduce.11.cloned.1.call-update) | async-done | bytes 16783376
  942.5 39.3 %psum.7 = f32[9,2]{0,1:T(2,128)S(1)} all-reduce(f32[9,2]{0,1:T(2,128)S(1)} %maximum_maximum_fusion), channel_id=1, replica_groups=mesh['task'=8,'samp'=4] {'task','samp'}, use_global_device_ids=true, to_apply=%region_35.36 | all-reduce | flops 18 | bytes 144 | tf_op jit(solution)/shard_map/psum | solution.py:333
  (320 shorter events, 266.7 us)
Async XLA Ops:
  7.2 198.7 %all-reduce.13.cloned.1.call-start = ((), (), s32[]{:S(2)}) async-start(), calls=%async_computation.3 | async-start | bytes 16789504
  21.7 286.8 %all-gather.2.cloned.1.call-start = ((), (), s32[]{:S(2)}) async-start(), calls=%async_computation.1 | async-start | bytes 5242880 | tf_op jit(solution)/shard_map/all_gather | solution.py:224
  24.8 183.8 %copy-start.57 = (f32[128,4]{0,1:T(4,128)}, f32[128,4]{0,1:T(4,128)S(1)}, u32[]{:S(2)}) copy-start(f32[128,4]{0,1:T(4,128)S(1)} %broadcast_multiply_fusion.2) | copy-start | bytes 6148
  25.1 180.8 %copy-start.63 = (f32[128,4]{0,1:T(4,128)}, f32[128,4]{0,1:T(4,128)S(1)}, u32[]{:S(2)}) copy-start(f32[128,4]{0,1:T(4,128)S(1)} %fusion.84) | copy-start | bytes 6148
  25.1 183.4 %copy-start.59 = (f32[128,4]{0,1:T(4,128)}, f32[128,4]{0,1:T(4,128)S(1)}, u32[]{:S(2)}) copy-start(f32[128,4]{0,1:T(4,128)S(1)} %fusion.106) | copy-start | bytes 6148
  313.2 20.1 %copy-start.34 = (bf16[512,512,1]{1,0,2:T(8,128)(2,1)S(1)}, bf16[512,512,1]{1,0,2:T(8,128)(2,1)}, u32[]{:S(2)}) copy-start(bf16[512,512,1]{1,0,2:T(8,128)(2,1)} %reshape.421) | copy-start | bytes 1572868
  334.9 8.8 copy-start.32
  360.5 27.2 %copy-start.7 = (f32[128,4,512]{2,0,1:T(8,128)}, f32[128,4,512]{2,0,1:T(8,128)S(1)}, u32[]{:S(2)}) copy-start(f32[128,4,512]{2,0,1:T(8,128)S(1)} %get-tuple-element.523) | copy-start | bytes 3145732
  362.3 12.4 %copy-start.33 = (bf16[2048,512]{1,0:T(8,128)(2,1)S(1)}, bf16[2048,512]{1,0:T(8,128)(2,1)}, u32[]{:S(2)}) copy-start(bf16[2048,512]{1,0:T(8,128)(2,1)} %slice.149) | copy-start | bytes 6291460
  362.3 12.4 %copy-start.55 = (bf16[512,512]{1,0:T(8,128)(2,1)S(1)}, bf16[512,512]{1,0:T(8,128)(2,1)}, u32[]{:S(2)}) copy-start(bf16[512,512]{1,0:T(8,128)(2,1)} %squeeze.65) | copy-start | bytes 1572868
  439.1 66.2 %reduce-scatter.6.cloned.1.call-start = ((), (), s32[]{:S(2)}) async-start(), calls=%async_computation.4 | async-start | bytes 2621440 | tf_op jit(solution)/shard_map/while
  509.3 67.2 %reduce-scatter.6.cloned.1.call-start = ((), (), s32[]{:S(2)}) async-start(), calls=%async_computation.4 | async-start | bytes 2621440 | tf_op jit(solution)/shard_map/while
  580.6 352.1 %all-reduce.11.cloned.1.call-start = ((), (), s32[]{:S(2)}) async-start(), calls=%async_computation.2 | async-start | bytes 33579008
  638.1 8.7 copy-start.9
  638.1 8.7 copy-start.24
  664.4 270.3 %copy-start.37 = (f32[65552]{0:T(1024)S(1)}, f32[65552]{0:T(1024)}, u32[]{:S(2)}) copy-start(f32[65552]{0:T(1024)} %get-tuple-element.510) | copy-start | bytes 786628
  666.0 317.4 %copy-start.52 = (f32[32784]{0:T(1024)S(1)}, f32[32784]{0:T(1024)}, u32[]{:S(2)}) copy-start(f32[32784]{0:T(1024)} %param.21) | copy-start | bytes 393412
  934.7 52.1 %copy-start.39 = (f32[65552]{0:T(1024)}, f32[65552]{0:T(1024)S(1)}, u32[]{:S(2)}) copy-start(f32[65552]{0:T(1024)S(1)} %get-tuple-element.491) | copy-start | bytes 786628
  934.7 52.1 %copy-start.40 = (f32[65552]{0:T(1024)}, f32[65552]{0:T(1024)S(1)}, u32[]{:S(2)}) copy-start(f32[65552]{0:T(1024)S(1)} %get-tuple-element.492) | copy-start | bytes 786628
  934.7 51.2 %copy-start.38 = (f32[65552]{0:T(1024)S(1)}, f32[65552]{0:T(1024)}, u32[]{:S(2)}) copy-start(f32[65552]{0:T(1024)} %param.27) | copy-start | bytes 786628
  937.2 49.5 %copy-start.48 = (f32[32784]{0:T(1024)}, f32[32784]{0:T(1024)S(1)}, u32[]{:S(2)}) copy-start(f32[32784]{0:T(1024)S(1)} %get-tuple-element.483) | copy-start | bytes 393412
  937.2 49.5 %copy-start.49 = (f32[32784]{0:T(1024)}, f32[32784]{0:T(1024)S(1)}, u32[]{:S(2)}) copy-start(f32[32784]{0:T(1024)S(1)} %get-tuple-element.484) | copy-start | bytes 393412
  939.1 47.6 %copy-start.50 = (f32[32784]{0:T(1024)}, f32[32784]{0:T(1024)S(1)}, u32[]{:S(2)}) copy-start(f32[32784]{0:T(1024)S(1)} %get-tuple-element.487) | copy-start | bytes 393412
  939.1 47.6 %copy-start.51 = (f32[32784]{0:T(1024)}, f32[32784]{0:T(1024)S(1)}, u32[]{:S(2)}) copy-start(f32[32784]{0:T(1024)S(1)} %get-tuple-element.488) | copy-start | bytes 393412
  (48 other events, 208.7 us)
Sparse Core Ops, SparseCore 0:
  21.8 184.0 all-reduce.12
  228.1 80.2 all-gather.1
  463.2 42.0 reduce-scatter.5
  533.3 43.1 reduce-scatter.5
  650.9 281.7 all-reduce.10
where the time goes:
time: 1000 us; the launch traced here: 994 us
  waiting for transfers between devices  568 us (57%)
  local copies, waits for them, and re-layouts  196 us (20%)
  matrix products  112 us (11%)
  other arithmetic  60.8 us (6%)
  blocking collectives  39.3 us (4%)
  between operations  16.3 us (2%)
    unnamed x5, waiting for transfers between devices  447 us
    while x4, waiting for transfers between devices  80.1 us
    all_gather x1, waiting for transfers between devices, on_device(): pairs_all = lax.all_gather(pairs_local, 'samp', axis=0, tiled=True)  40.5 us
    psum x1, blocking collectives, on_device(): lax.psum(jnp.concatenate([sample_state[4], feature_state[4], mlp_state[4]...  39.3 us
    while x12, local copies, waits for them, and re-layouts  38.6 us
    unnamed x145, local copies, waits for them, and re-layouts  29.9 us
    reshape x6, local copies, waits for them, and re-layouts, unpack(): w_in = flat_params[D:D + D * width_in].reshape(D, width_in)  22.5 us
  transfers between devices with their start and end apart: 5, of which 5 were waited for; matrix products, arithmetic and copies ran while one was open for 6% of the time, Pallas kernels for 0%

commit v1 on v0

--- a/solution.py
+++ b/solution.py
@@ -1,6 +1,8 @@
 import jax
 import jax.numpy as jnp
 from jax import lax
+from jax.experimental import pallas as pl
+from jax.experimental.pallas import tpu as pltpu
 from jax.sharding import PartitionSpec as P
 
 D = 512
@@ -360,6 +362,1049 @@
     )
 
 
+D = 512
+MESH = pl.DeviceIdType.MESH
+BF = jnp.bfloat16
+F32 = jnp.float32
+NEG = -1e30
+
+
+def mult(value, factor):
+    return value if isinstance(value, int) else pl.multiple_of(value, factor)
+
+
+def nt(left, right):
+    return lax.dot_general(left, right, (((1,), (1,)), ((), ())), preferred_element_type=F32)
+
+
+def nn(left, right):
+    return lax.dot_general(left, right, (((1,), (0,)), ((), ())), preferred_element_type=F32)
+
+
+def here():
+    return lax.axis_index("task"), lax.axis_index("samp")
+
+
+def peers(t, s):
+    return [(jnp.bitwise_xor(t, e), s) for e in range(1, 8)] + [(t, jnp.bitwise_xor(s, e)) for e in (1, 2, 3)]
+
+
+def enter(t, s):
+    barrier = pltpu.get_barrier_semaphore()
+    for peer in peers(t, s):
+        pl.semaphore_signal(barrier, inc=1, device_id=peer, device_id_type=MESH)
+    return barrier
+
+
+def send(src, dst, ssem, rsem, peer):
+    copy = pltpu.make_async_remote_copy(
+        src_ref=src, dst_ref=dst, send_sem=ssem, recv_sem=rsem, device_id=peer, device_id_type=MESH
+    )
+    copy.start()
+    return copy
+
+
+class Gather:
+    def __init__(self, buf, ssem, rsem, t, s):
+        self.buf, self.t, self.s = buf, t, s
+        half = buf.shape[2] // 2
+        self.ha, self.hb, self.all = pl.ds(0, half), pl.ds(half, half), pl.ds(0, 2 * half)
+        self.rows = pl.ds(0, buf.shape[1])
+        self.ssem, self.rsem = ssem, rsem
+        self.moves = []
+        self.tx, self.ty = jnp.bitwise_xor(t, 2), jnp.bitwise_xor(t, 4)
+        self.txy, self.tc = jnp.bitwise_xor(t, 6), jnp.bitwise_xor(t, 1)
+        self.hops, self.sent = {}, {k: {} for k in ("x", "y", "c", "xy", "yx", "cx", "cy")}
+
+    def z(self, key):
+        return jnp.bitwise_xor(self.s, key)
+
+    def go(self, slots, cols, peer):
+        view = self.buf.at[slots, self.rows, cols]
+        i = len(self.moves)
+        copy = send(view, view, self.ssem.at[i], self.rsem.at[i], peer)
+        self.moves.append(copy)
+        return copy
+
+    def pass_on(self, kind, key, t, cols, to):
+        self.sent[kind][key] = self.go(pl.ds(4 * t + self.z(key), 1), cols, (to, self.s))
+
+    def spread(self, key):
+        self.pass_on("x", key, self.t, self.all, self.tx)
+        self.pass_on("y", key, self.t, self.all, self.ty)
+        self.pass_on("c", key, self.t, self.all, self.tc)
+
+    def hop(self, key, slot, to):
+        self.hops[key] = self.go(pl.ds(4 * self.t + self.z(slot), 1), self.all, (self.t, self.z(to)))
+
+    def start_z(self):
+        self.hop(2, 0, 2)
+        self.hop(1, 0, 1)
+
+    def zin(self, *keys):
+        for key in keys:
+            self.hops[key].wait_recv()
+            if key == 2:
+                self.hop(3, 2, 1)
+            self.spread(key)
+
+    def near(self, *keys):
+        for key in keys:
+            self.sent["x"][key].wait_recv()
+            self.pass_on("xy", key, self.tx, self.ha, self.ty)
+            self.pass_on("cx", key, self.tx, self.all, self.tc)
+            self.sent["y"][key].wait_recv()
+            self.pass_on("yx", key, self.ty, self.hb, self.tx)
+            self.pass_on("cy", key, self.ty, self.all, self.tc)
+
+    def far(self):
+        for kind in ("xy", "yx"):
+            for copy in self.sent[kind].values():
+                copy.wait_recv()
+        self.last = self.go(pl.ds(4 * self.txy, 4), self.all, (self.tc, self.s))
+
+    def end(self):
+        for kind in ("c", "cx", "cy"):
+            for copy in self.sent[kind].values():
+                copy.wait_recv()
+        self.last.wait_recv()
+
+    def drain(self):
+        for copy in self.moves:
+            copy.wait_send()
+
+
+def realign(m_ref, sh_ref, d, rows, out_ref, out_at, roll_to):
+    whole = 4 * rows
+    total = whole + 8
+    q, p = d // 8, d % 8
+    lane = lax.broadcasted_iota(jnp.int32, (total, 128), 1)
+    roll_to[0:8, :] = jnp.zeros((8, 128), F32)
+    for i in range(whole // 8):
+        sh_ref[8 * i : 8 * i + 8, :] = m_ref[pl.ds(1024 * i, 1024)].reshape(8, 128)
+    sh_ref[whole:total, :] = jnp.zeros((8, 128), F32)
+    sh_ref[whole : whole + 1, 0:16] = m_ref[pl.ds(128 * whole, 16)].reshape(1, 16)
+    rolled = pltpu.roll(sh_ref[0:total, :], 16 * p, 1)
+    roll_to[8 : 8 + total, :] = rolled
+    sh_ref[0:8, :] = jnp.zeros((8, 128), F32)
+    sh_ref[8 : 8 + total, :] = jnp.where(lane < 16 * p, roll_to[7 : 7 + total, :], rolled)
+    firsts = []
+    for b in range(4):
+        out_ref[out_at, 0:rows, 128 * b : 128 * b + 128] = sh_ref[pl.ds(12 - q + b, rows, stride=4), :].astype(BF)
+        firsts.append(sh_ref[pl.ds(8 - q + b, 1), :])
+    return jnp.concatenate(firsts, 1)
+
+
+def spread(buf, firsts, kind, rows, lo, hi, put):
+    tail = lax.broadcasted_iota(jnp.int32, (8, D), 0) == 7
+
+    def body(i, _):
+        nxt = jnp.minimum(i + 1, 31)
+        row = firsts[nxt, :, D * kind : D * kind + D]
+        block = buf[i, 0:rows, :].astype(F32)
+        last = block[rows - 8 : rows, :] + jnp.where(tail & (i < 31), row, 0.0)
+        put(i - lo, block[0 : rows - 8, :], last)
+        return 0
+
+    lax.fori_loop(lo, hi, body, 0)
+
+
+def put_f32(dst, rows):
+    def put(i, head, last):
+        for b in range(4):
+            cols = slice(128 * b, 128 * b + 128)
+            dst[b, pl.ds(mult(i * rows, rows), rows - 8), :] = head[:, cols]
+            dst[b, pl.ds(mult(i * rows + rows - 8, 8), 8), :] = last[:, cols]
+
+    return put
+
+
+def put_bf(dst, rows):
+    def put(i, head, last):
+        dst[pl.ds(mult(i * rows, rows), rows), :] = jnp.concatenate([head, last], 0).astype(BF)
+
+    return put
+
+
+def split_columns(wide, ways, dst):
+    def body(i, _):
+        for j in range(ways):
+            for b in range(4):
+                piece = wide[b, pl.ds(64 * ways * i + j, 64, stride=ways), :]
+                dst[j, pl.ds(mult(64 * i, 64), 64), 128 * b : 128 * b + 128] = piece.astype(BF)
+        return 0
+
+    lax.fori_loop(0, 8, body, 0)
+
+
+def halves():
+    lane = lax.broadcasted_iota(jnp.int32, (128, 128), 1)
+    return lane < 64
+
+
+def two_heads(x, one, two):
+    return jnp.concatenate([x * one, x * two], 0)
+
+
+def soft(scores, axis):
+    e = [jnp.exp(x - jnp.max(x, axis, keepdims=True)) for x in scores]
+    return [x * (1.0 / jnp.sum(x, axis, keepdims=True)) for x in e]
+
+
+def attend_chunk(qkv, c, live, out):
+    left = halves()
+    one = jnp.where(left, 0.125, 0.0).astype(BF)
+    two = jnp.where(left, 0.0, 0.125).astype(BF)
+    rows = pl.ds(mult(c * 128, 128), 128)
+
+    def body(h, _):
+        cols = [pl.ds(128 * i, 128) for i in range(4)]
+        scores = [jnp.where(live, nt(two_heads(qkv[0, rows, w], one, two), qkv[1, :, w]), NEG) for w in cols]
+        prob = [p.astype(BF) for p in soft(scores, 1)]
+        outs = [nn(p, qkv[2, :, w]) for p, w in zip(prob, cols)]
+        for o, w in zip(outs, cols):
+            o = jnp.where(left, o[0:128], o[128:256]).astype(BF)
+            for g in range(4):
+                out[g, :, w] = o[32 * g : 32 * g + 32]
+        return 0
+
+    body(0, 0)
+
+
+def edges(d, entries, width):
+    begin = d * entries
+    return D - begin, D + D * width - begin
+
+
+def segment(k, ends):
+    return (k >= ends[0]).astype(jnp.int32) + (k >= ends[1]).astype(jnp.int32)
+
+
+def lamb_step(g, m, f, s):
+    fn = 0.5 * f + 0.5 * g
+    sn = 0.5 * s + 0.5 * g * g
+    return fn, sn, fn / (jnp.sqrt(sn) + 1e-6)
+
+
+def flat_index():
+    rows = lax.broadcasted_iota(jnp.int32, (32, 128), 0)
+    return rows * 128 + lax.broadcasted_iota(jnp.int32, (32, 128), 1)
+
+
+def fold(x):
+    return x.reshape(-1, 8, 128).sum(0)
+
+
+def squares(sh, m, f, s, sums, d, width, b, lo, hi):
+    entries = m.shape[0]
+    ends = edges(d, entries, width)
+    index = flat_index()
+
+    def body(i, acc):
+        at = pl.ds(mult(i * 4096, 4096), 4096)
+        old = m[at].reshape(32, 128)
+        _, _, r = lamb_step(sh[pl.ds(mult(i * 32, 32), 32), :], old, f[at].reshape(32, 128), s[at].reshape(32, 128))
+        part = segment(index + i * 4096, ends)
+        out = []
+        for n, value in enumerate((old * old, r * r)):
+            for k in range(3):
+                out.append(acc[3 * n + k] + fold(jnp.where(part == k, value, 0.0)))
+        return tuple(out)
+
+    acc = lax.fori_loop(lo, hi, body, (jnp.zeros((8, 128), F32),) * 6)
+    for n in range(2):
+        for k in range(3):
+            row = 16 * n + 3 * b + k
+            sums[row : row + 1, :] += jnp.sum(acc[3 * n + k], 0, keepdims=True)
+
+
+def squares_tail(sh, m, f, s, sums, d, width, b):
+    entries = m.shape[0]
+    base = entries - 16
+    ends = edges(d, entries, width)
+    at = pl.ds(base, 16)
+    old = m[at].reshape(1, 16)
+    row = base // 128
+    _, _, r = lamb_step(sh[row : row + 1, 0:16], old, f[at].reshape(1, 16), s[at].reshape(1, 16))
+    part = segment(lax.broadcasted_iota(jnp.int32, (1, 16), 1) + base, ends)
+    for n, value in enumerate((old * old, r * r)):
+        for k in range(3):
+            row = 16 * n + 3 * b + k
+            sums[row : row + 1, 0:16] += jnp.where(part == k, value, 0.0)
+
+
+def update(sh, m, f, s, grad, fout, sout, mout, wout, ratio, d, width, b):
+    entries = m.shape[0]
+    whole = entries // 4096
+    ends = edges(d, entries, width)
+    half = [0.5 * ratio[3 * b + k : 3 * b + k + 1, :] for k in range(3)]
+
+    def put(at, g, part, shape):
+        old = m[at].reshape(shape)
+        fn, sn, r = lamb_step(g, old, f[at].reshape(shape), s[at].reshape(shape))
+        factor = jnp.where(part == 0, half[0], jnp.where(part == 1, half[1], half[2]))
+        new = (old - factor * r).reshape(-1)
+        grad[at] = g.reshape(-1)
+        fout[at] = fn.reshape(-1)
+        sout[at] = sn.reshape(-1)
+        mout[at] = new
+        wout[at] = new.astype(BF)
+
+    index = flat_index()
+
+    def body(i, _):
+        at = pl.ds(mult(i * 4096, 4096), 4096)
+        put(at, sh[pl.ds(mult(i * 32, 32), 32), :], segment(index + i * 4096, ends), (32, 128))
+        return 0
+
+    lax.fori_loop(0, whole, body, 0)
+    part = segment(lax.broadcasted_iota(jnp.int32, (1, 16), 1) + whole * 4096, ends)
+    put(pl.ds(whole * 4096, 16), sh[32 * whole : 32 * whole + 1, 0:16], part, (1, 16))
+
+
+def diagonal(rows):
+    lane = lax.broadcasted_iota(jnp.int32, (32, 128), 1)
+    return lane == lax.broadcasted_iota(jnp.int32, (32, 128), 0)
+
+
+def sum_all(sums, ts, zs, ssem, rsem, t, s):
+    column = jnp.sum(sums[...], 1, keepdims=True)
+    ts[t] = jnp.broadcast_to(jnp.sum(jnp.where(diagonal(32), column, 0.0), 0, keepdims=True), (8, 128))
+    plane = [
+        send(ts.at[t], ts.at[t], ssem.at[e - 1], rsem.at[e - 1], (jnp.bitwise_xor(t, e), s)) for e in range(1, 8)
+    ]
+    for copy in plane:
+        copy.wait_recv()
+    zs[s] = ((ts[0] + ts[1]) + (ts[2] + ts[3])) + ((ts[4] + ts[5]) + (ts[6] + ts[7]))
+    last = [
+        send(zs.at[s], zs.at[s], ssem.at[6 + e], rsem.at[6 + e], (t, jnp.bitwise_xor(s, e))) for e in (1, 2, 3)
+    ]
+    for copy in last:
+        copy.wait_recv()
+    return (zs[0] + zs[1]) + (zs[2] + zs[3]), plane + last
+
+
+def kernel_e(
+    total, sh1, sh2, sh3, m1, f1, s1, m2, f2, s2, m3, f3, s3,
+    g1, fo1, so1, mo1, wo1, g2, fo2, so2, mo2, wo2, g3, fo3, so3, mo3, wo3, pairs,
+):
+    t, s = here()
+    d = 4 * t + s
+    norm = jnp.sqrt(jnp.sum(jnp.where(diagonal(32), total[0:1, :], 0.0), 1, keepdims=True))
+    pairs[...] = jnp.concatenate([norm[0:9], norm[16:25]], 1)
+    ratio = norm[0:9] / (norm[16:25] + 1e-6)
+    update(sh1, m1, f1, s1, g1, fo1, so1, mo1, wo1, ratio, d, 3 * D, 0)
+    update(sh2, m2, f2, s2, g2, fo2, so2, mo2, wo2, ratio, d, 3 * D, 1)
+    update(sh3, m3, f3, s3, g3, fo3, so3, mo3, wo3, ratio, d, 4 * D, 2)
+
+
+def call_e(total, shards, args):
+    sds = jax.ShapeDtypeStruct
+    vm = pl.BlockSpec(memory_space=pltpu.VMEM)
+    shapes = []
+    for m in args[0::3]:
+        n = m.shape
+        shapes += [sds(n, F32)] * 4 + [sds(n, BF)]
+    return pl.pallas_call(
+        kernel_e,
+        name="kernel_e",
+        out_shape=(*shapes, sds((9, 2), F32)),
+        in_specs=[vm] * 13,
+        out_specs=(vm,) * 16,
+        compiler_params=pltpu.CompilerParams(vmem_limit_bytes=40 << 20),
+    )(total, *shards, *args)
+
+
+def backward_heads(h, qkv, do, live, dqkv, kt, dkv):
+    left = halves()
+    one, two = jnp.where(left, 1.0, 0.0).astype(BF), jnp.where(left, 0.0, 1.0).astype(BF)
+    cols = pl.ds(mult(h * 128, 128), 128)
+    kt[...] = jnp.transpose(qkv[1, :, cols])
+    top_lane = lax.broadcasted_iota(jnp.int32, (128, 128), 0) < 64
+
+    def chunk(n, _):
+        each = [0, 1, 2, 3]
+        rows = [pl.ds(c * 128, 128) for c in each]
+        qm = [two_heads(qkv[0, r, cols] * jnp.asarray(0.125, BF), one, two) for r in rows]
+        gm = [two_heads(do[c, :, :, cols].reshape(128, 128), one, two) for c in each]
+        prob = soft([jnp.where(live, nt(qkv[1, :, cols], q), NEG) for q in qm], 0)
+        pg = [nt(qkv[2, :, cols], g) for g in gm]
+        sg = [(p * (x - jnp.sum(p * x, 0, keepdims=True))).astype(BF) for p, x in zip(prob, pg)]
+        dqkv[1, :, cols] = (nn(sg[0], qm[0]) + nn(sg[1], qm[1]) + nn(sg[2], qm[2]) + nn(sg[3], qm[3])).astype(BF)
+        pb = [p.astype(BF) for p in prob]
+        dqkv[2, :, cols] = (nn(pb[0], gm[0]) + nn(pb[1], gm[1]) + nn(pb[2], gm[2]) + nn(pb[3], gm[3])).astype(BF)
+        for r, x in zip(rows, sg):
+            dqt = nn(kt[...], x)
+            dq = jnp.transpose(jnp.where(top_lane, dqt[:, 0:128], dqt[:, 128:256])) * 0.125
+            dqkv[0, r, cols] = dq.astype(BF)
+        return 0
+
+    chunk(0, 0)
+
+
+def turn(x):
+    return jnp.transpose(x)
+
+
+def stats(h):
+    x = h - jnp.mean(h, 1, keepdims=True)
+    rstd = lax.rsqrt(jnp.mean(x * x, 1, keepdims=True) + 1e-5)
+    return x * rstd, rstd
+
+
+def norm_grad(h, da, gain):
+    x, rstd = stats(h)
+    dgain = jnp.sum(da * x, 0, keepdims=True)
+    dx = da * gain
+    dh = rstd * (dx - jnp.mean(dx, 1, keepdims=True) - x * jnp.mean(dx * x, 1, keepdims=True))
+    return dh, dgain
+
+
+def block(g):
+    return pl.ds(mult(g * 128, 128), 128)
+
+
+def feature_mask(fcnt, axis):
+    shape = (256, 128) if axis else (128, 256)
+    query = lax.broadcasted_iota(jnp.int32, shape, 1 - axis)
+    key = lax.broadcasted_iota(jnp.int32, shape, axis)
+    return (query % 32 == key % 32) & (key // 32 < fcnt)
+
+
+def feature_forward(qkv, o2, fcnt):
+    left = halves()
+    one = jnp.where(left, 0.125, 0.0).astype(BF)
+    two = jnp.where(left, 0.0, 0.125).astype(BF)
+    ok = feature_mask(fcnt, 1)
+    cols = [slice(128 * h, 128 * h + 128) for h in range(4)]
+
+    def body(n, _):
+        rows = block(n)
+        scores = [
+            jnp.where(ok, nt(two_heads(qkv[0, rows, c], one, two), qkv[1, rows, c]), NEG) for c in cols
+        ]
+        prob = [p.astype(BF) for p in soft(scores, 1)]
+        out = [nn(p, qkv[2, rows, c]) for p, c in zip(prob, cols)]
+        for o, c in zip(out, cols):
+            o2[rows, c] = jnp.where(left, o[0:128], o[128:256]).astype(BF)
+        return 0
+
+    lax.fori_loop(0, 4, body, 0)
+
+
+def feature_backward(qkv, do, dqkv, fcnt):
+    left = halves()
+    one, two = jnp.where(left, 1.0, 0.0).astype(BF), jnp.where(left, 0.0, 1.0).astype(BF)
+    ok = feature_mask(fcnt, 0)
+    top_lane = lax.broadcasted_iota(jnp.int32, (128, 128), 0) < 64
+    cols = [slice(128 * h, 128 * h + 128) for h in range(4)]
+
+    def body(n, _):
+        rows = block(n)
+        qm = [two_heads(qkv[0, rows, c] * jnp.asarray(0.125, BF), one, two) for c in cols]
+        gm = [two_heads(do[rows, c], one, two) for c in cols]
+        prob = soft([jnp.where(ok, nt(qkv[1, rows, c], q), NEG) for c, q in zip(cols, qm)], 0)
+        pg = [nt(qkv[2, rows, c], g) for c, g in zip(cols, gm)]
+        sg = [(p * (x - jnp.sum(p * x, 0, keepdims=True))).astype(BF) for p, x in zip(prob, pg)]
+        dqt = [nn(turn(qkv[1, rows, c]), x) for c, x in zip(cols, sg)]
+        dk = [nn(x, q).astype(BF) for x, q in zip(sg, qm)]
+        dv = [nn(p.astype(BF), g).astype(BF) for p, g in zip(prob, gm)]
+        dq = [turn(jnp.where(top_lane, x[:, 0:128], x[:, 128:256])) * 0.125 for x in dqt]
+        for i, c in enumerate(cols):
+            dqkv[0, rows, c] = dq[i].astype(BF)
+            dqkv[1, rows, c] = dk[i]
+            dqkv[2, rows, c] = dv[i]
+        return 0
+
+    lax.fori_loop(0, 4, body, 0)
+
+
+def four_blocks(body, init=0):
+    for r in range(4):
+        init = body(r, init)
+    return init
+
+
+def flat(x):
+    return x.reshape(128, D)
+
+
+def cube(x):
+    return x.reshape(4, 32, D)
+
+
+def narrow_to(wide, part, slots, rows):
+    def body(i, _):
+        at = pl.ds(mult(i * rows, rows), rows)
+        for b in range(4):
+            part[i, :, 128 * b : 128 * b + 128] = wide[b, at, :].astype(BF)
+        return 0
+
+    lax.fori_loop(0, slots, body, 0)
+
+
+def store_wide(wide, j, ways, value):
+    for b in range(4):
+        wide[b, pl.ds(j, value.shape[0], stride=ways), :] = value[:, 128 * b : 128 * b + 128]
+
+
+def mlp(a3, a3t, g, h2, wup, wdn, h3, da, zb, dub, u, dz, wide, p3):
+    h3[...] = h2[...]
+    da[...] = jnp.zeros((512, D), F32)
+
+    def body(j, _):
+        u[...] = nn(a3[...], wup[j])
+        dz[...] = nt(g[...], wdn[j]).astype(BF)
+
+        def act(r, _):
+            rows = pl.ds(mult(r * 64, 64), 64)
+            x = u[rows, :]
+            cdf = 0.5 * (1.0 + lax.erf(x * 0.7071067811865476))
+            zb[rows, :] = (x * cdf).astype(BF)
+            slope = cdf + x * (0.3989422804014327 * jnp.exp(-0.5 * x * x))
+            dub[rows, :] = (slope * dz[rows, :].astype(F32)).astype(BF)
+            return 0
+
+        lax.fori_loop(0, 8, act, 0)
+        h3[...] += nn(zb[...], wdn[j])
+        da[...] += nt(dub[...], wup[j])
+        store_wide(wide, j, 4, nn(a3t[...], dub[...]))
+        dw = nn(turn(zb[...]), g[...]).astype(BF)
+        for i in range(4):
+            p3[16 + 4 * j + i] = dw[128 * i : 128 * i + 128]
+        return 0
+
+    lax.fori_loop(0, 4, body, 0)
+    narrow_to(wide, p3, 16, 128)
+
+
+def middle_forward(s, cells, top, o1, wo1, w2, wo2, gains, scnt, fcnt, h1, h2, a2, qkv, o2, a3, g):
+    gain2, gain3 = gains[1:2, :], gains[2:3, :]
+    h1[...] = nn(o1[...].reshape(512, D), wo1[...])
+
+    def first(r, _):
+        rows = block(r)
+        h = h1[rows, :] + flat(cells[r].astype(F32))
+        h1[rows, :] = h
+        x, _ = stats(h)
+        a2[rows, :] = (x * gain2).astype(BF)
+        n = lax.broadcasted_iota(jnp.int32, (128, 1), 0)
+        live = (n // 32 < fcnt) & (128 * s + 32 * r + n % 32 < scnt)
+        g[rows, :] = jnp.where(live, flat(top[r].astype(F32)), 0.0).astype(BF)
+        return 0
+
+    four_blocks(first)
+
+    def project(j, _):
+        qkv[j] = nn(a2[...], w2[j]).astype(BF)
+        return 0
+
+    lax.fori_loop(0, 3, project, 0)
+    feature_forward(qkv, o2, fcnt)
+    h2[...] = h1[...] + nn(o2[...], wo2[...])
+
+    def second(r, _):
+        rows = block(r)
+        x, _ = stats(h2[rows, :])
+        a3[rows, :] = (x * gain3).astype(BF)
+        return 0
+
+    four_blocks(second)
+
+
+def layer_output(s, h3, lout, scnt, fcnt):
+    def last(r, _):
+        n = lax.broadcasted_iota(jnp.int32, (128, 1), 0)
+        live = (n // 32 < fcnt) & (128 * s + 32 * r + n % 32 < scnt)
+        lout[r] = cube(jnp.where(live, h3[block(r), :], 0.0).astype(BF))
+        return 0
+
+    four_blocks(last)
+
+
+def feature_grads(wo1, w2, wo2, gains, fcnt, h1, h2, qkv, g, da, b2, b1, do, dqkv, do1, gr, dgain, hook):
+    gain2, gain3 = gains[1:2, :], gains[2:3, :]
+
+    def third(r, dg):
+        rows = block(r)
+        dh, part = norm_grad(h2[rows, :], da[rows, :], gain3)
+        total = g[rows, :].astype(F32) + dh
+        gr[r] = cube(total)
+        b2[rows, :] = total.astype(BF)
+        return dg + part
+
+    dg3 = four_blocks(third, jnp.zeros((1, D), F32))
+    do[...] = nt(b2[...], wo2[...]).astype(BF)
+    feature_backward(qkv, do, dqkv, fcnt)
+    hook()
+    da[...] = nt(dqkv[0], w2[0]) + nt(dqkv[1], w2[1]) + nt(dqkv[2], w2[2])
+
+    def fourth(r, dg):
+        rows = block(r)
+        dh, part = norm_grad(h1[rows, :], da[rows, :], gain2)
+        total = flat(gr[r]) + dh
+        gr[r] = cube(total)
+        b1[rows, :] = total.astype(BF)
+        return dg + part
+
+    dg2 = four_blocks(fourth, jnp.zeros((1, D), F32))
+    do1[...] = nt(b1[...], wo1[...]).astype(BF).reshape(4, 4, 32, D)
+    n = lax.broadcasted_iota(jnp.int32, (8, D), 0)
+    dgain[...] = jnp.where(n == 1, dg2, jnp.where(n == 2, dg3, 0.0))
+
+
+def feature_weights(o1, a2, o2, b2, b1, dqkv, wide, p2, dwo1):
+    def weights(j, _):
+        store_wide(wide, j, 3, nn(turn(a2[...]), dqkv[j]))
+        return 0
+
+    lax.fori_loop(0, 3, weights, 0)
+    narrow_to(wide, p2, 24, 64)
+    dw = nn(turn(o2[...]), b2[...]).astype(BF)
+    for i in range(8):
+        p2[24 + i] = dw[64 * i : 64 * i + 64]
+    dwo1[...] = nn(turn(o1[...].reshape(512, D)), b1[...]).astype(BF)
+
+
+class Reduce:
+    def __init__(self, part, r1, ry, rx, ry2, rx2, rz, ssem, rsem, t, s):
+        self.part, self.r1 = part, r1
+        self.ry, self.rx, self.ry2, self.rx2, self.rz = ry, rx, ry2, rx2, rz
+        half = part.shape[2] // 2
+        self.ha, self.hb, self.all = pl.ds(0, half), pl.ds(half, half), pl.ds(0, 2 * half)
+        self.ssem, self.rsem, self.t, self.s = ssem, rsem, t, s
+        self.copies = []
+
+    def go(self, src, dst, peer):
+        i = len(self.copies)
+        copy = send(src, dst, self.ssem.at[i], self.rsem.at[i], peer)
+        self.copies.append(copy)
+        return copy
+
+    def xor(self, e):
+        return jnp.bitwise_xor(self.t, e)
+
+    def group(self, e, cols):
+        return self.part.at[pl.ds(4 * self.xor(2 * e), 4), :, cols]
+
+    def core(self):
+        tc = self.xor(1)
+        self.c = [
+            self.go(self.part.at[pl.ds(4 * jnp.bitwise_xor(tc, 2 * e), 4)], self.r1.at[e], (tc, self.s))
+            for e in (2, 3, 1, 0)
+        ]
+
+    def add(self, e, cols, got):
+        base = 4 * self.xor(2 * e)
+        for j in range(4):
+            own = self.part[base + j, :, cols].astype(F32)
+            self.part[base + j, :, cols] = (own + got[j].astype(F32)).astype(self.part.dtype)
+
+    def one(self):
+        ty, tx, s = self.xor(4), self.xor(2), self.s
+        self.y, self.x = {}, {}
+        for n, e in enumerate((2, 3, 1, 0)):
+            self.c[n].wait_recv()
+            self.add(e, self.all, self.r1.at[e])
+            if e in (2, 3):
+                self.y[e - 2] = self.go(self.group(e, self.ha), self.ry.at[e - 2], (ty, s))
+            if e in (3, 1):
+                self.x[e // 2] = self.go(self.group(e, self.hb), self.rx.at[e // 2], (tx, s))
+
+    def two(self):
+        ty, tx, s = self.xor(4), self.xor(2), self.s
+        self.y[1].wait_recv()
+        self.add(1, self.ha, self.ry.at[1])
+        self.x2 = self.go(self.group(1, self.ha), self.rx2, (tx, s))
+        self.x[1].wait_recv()
+        self.add(2, self.hb, self.rx.at[1])
+        self.y2 = self.go(self.group(2, self.hb), self.ry2, (ty, s))
+        self.y[0].wait_recv()
+        self.add(0, self.ha, self.ry.at[0])
+        self.x[0].wait_recv()
+        self.add(0, self.hb, self.rx.at[0])
+
+    def three(self):
+        self.x2.wait_recv()
+        self.add(0, self.ha, self.rx2)
+        self.y2.wait_recv()
+        self.add(0, self.hb, self.ry2)
+        self.z = [self.z_send(1, 0), self.z_send(3, 1)]
+
+    def z_send(self, slot, into):
+        t, s = self.t, self.s
+        to = jnp.bitwise_xor(s, 2 if into == 2 else 1)
+        return self.go(self.part.at[4 * t + jnp.bitwise_xor(s, slot)], self.rz.at[into], (t, to))
+
+    def four(self):
+        self.z[1].wait_recv()
+        mine = 4 * self.t + jnp.bitwise_xor(self.s, 2)
+        own = self.part[mine, :, :].astype(F32)
+        self.part[mine, :, :] = (own + self.rz[1, :, :].astype(F32)).astype(self.part.dtype)
+        self.z.append(self.z_send(2, 2))
+
+    def result(self):
+        self.z[0].wait_recv()
+        self.z[2].wait_recv()
+        own = self.part[4 * self.t + self.s, :, :].astype(F32)
+        return own + self.rz[0, :, :].astype(F32) + self.rz[2, :, :].astype(F32)
+
+    def drain(self):
+        for copy in self.copies:
+            copy.wait_send()
+
+
+def edge_rows(part, edges, kind):
+    rows = part.shape[1]
+
+    def body(i, _):
+        row = part[i - 1, rows - 16 : rows, :].astype(F32)[15:16, :]
+        edges[i, :, D * kind : D * kind + D] = row
+        return 0
+
+    lax.fori_loop(1, 32, body, 0)
+
+
+def to_rows(main, fl):
+    rows = main.shape[0]
+    for b in range(4):
+        fl[pl.ds(4 + b, rows, stride=4), :] = main[:, 128 * b : 128 * b + 128]
+
+
+def first_row(row, fl):
+    for b in range(4):
+        fl[b : b + 1, :] = row[:, 128 * b : 128 * b + 128]
+
+
+def shifted(fl, d, total):
+    q, p = d // 8, d % 8
+    back = (128 - 16 * p) % 128
+    lane = lax.broadcasted_iota(jnp.int32, (total, 128), 1)
+    low = pltpu.roll(fl[pl.ds(q, total), :], back, 1)
+    high = pltpu.roll(fl[pl.ds(q + 1, total), :], back, 1)
+    return jnp.where(lane < 128 - 16 * p, low, high)
+
+
+def to_shard(fl, rows, d, out_ref):
+    total = out_ref.shape[0]
+    fl[4 + 4 * rows : total + 8, :] = jnp.zeros((total + 4 - 4 * rows, 128), F32)
+    out_ref[...] = shifted(fl, d, total)
+
+
+def top_shard(fl, d, out_ref):
+    out_ref[0:8, :] = shifted(fl, d, 8)
+
+
+class Refs:
+    def __init__(self, names, refs):
+        for name, ref in zip(names, refs, strict=True):
+            setattr(self, name, ref)
+
+
+def reduce_names(n):
+    return [k + n for k in ("r1", "ry", "rx", "ry2", "rx2", "rz")]
+
+
+def reduce_scratch(rows, width=D, kind=BF):
+    half = width // 2
+    return [
+        pltpu.VMEM((4, 4, rows, width), kind), pltpu.VMEM((2, 4, rows, half), kind),
+        pltpu.VMEM((2, 4, rows, half), kind), pltpu.VMEM((4, rows, half), kind), pltpu.VMEM((4, rows, half), kind),
+        pltpu.VMEM((3, rows, width), kind),
+    ]
+
+
+PARAMS = ["m1", "f1", "s1", "m2", "f2", "s2", "m3", "f3", "s3"]
+WIDE = pltpu.VMEM((D, D), F32)
+NARROW = pltpu.VMEM((D, D), BF)
+THREE = pltpu.VMEM((3, D, D), BF)
+FOUR = pltpu.VMEM((4, D, D), BF)
+TILE = pltpu.VMEM((4, 4, 32, D), BF)
+DMA = pltpu.SemaphoreType.DMA
+SCRATCH = {
+    "g1": pltpu.VMEM((32, 64, D), BF), "ge": pltpu.VMEM((32, 1, 3 * D), F32), "g2": pltpu.VMEM((32, 64, D), BF), "g3": pltpu.VMEM((32, 128, D), BF),
+    "wide": pltpu.VMEM((4, 4 * D, 128), F32), "sh": pltpu.VMEM((536, 128), F32), "ro": pltpu.VMEM((536, 128), F32),
+    "w1": THREE, "wo1": NARROW, "w2": THREE, "wo2": NARROW, "wup": FOUR, "wdn": FOUR,
+    "gains": pltpu.VMEM((8, D), F32), "dgain": pltpu.VMEM((8, D), F32),
+    "cf": TILE, "a1": NARROW, "qkv1": THREE, "o1c": pltpu.VMEM((3, 4, 32, D), BF), "o1": TILE,
+    "h1": WIDE, "h2": WIDE, "a2": NARROW, "qkv2": THREE, "o2": NARROW, "a3": NARROW, "at": NARROW, "g": NARROW,
+    "h3": WIDE, "da": WIDE, "zb": NARROW, "dub": NARROW, "u": WIDE, "dz": NARROW, "b": NARROW, "b1": NARROW, "do2": NARROW,
+    "dqkv": THREE, "gr": pltpu.VMEM((4, 4, 32, D), F32), "do1": TILE, "do": TILE, "dwo1": NARROW,
+    "kt": pltpu.VMEM((128, D), BF), "dkv": pltpu.VMEM((2, D, 128), F32), "dhs": TILE, "dhr": TILE,
+    **dict(zip(reduce_names("a"), reduce_scratch(64))),
+    **dict(zip(reduce_names("b"), reduce_scratch(64))),
+    **dict(zip(reduce_names("c"), reduce_scratch(128))),
+    **dict(zip(reduce_names("d"), reduce_scratch(1, 3 * D, F32))),
+    "fl1": pltpu.VMEM((272, 128), F32), "fl2": pltpu.VMEM((272, 128), F32), "fl3": pltpu.VMEM((528, 128), F32),
+    "sums": pltpu.VMEM((32, 128), F32), "ts": pltpu.VMEM((8, 8, 128), F32), "zs": pltpu.VMEM((4, 8, 128), F32),
+    "gs": DMA((4, 32)), "gq": DMA((4, 32)), "rs": DMA((4, 16)), "rq": DMA((4, 16)),
+    "as1": DMA((3,)), "aq1": DMA((3,)), "as2": DMA((3,)), "aq2": DMA((3,)),
+    "as3": DMA((3,)), "aq3": DMA((3,)), "as4": DMA((3,)), "aq4": DMA((3,)), "ns": DMA((10,)), "nq": DMA((10,)),
+}
+INPUTS = ["scnt", "fcnt", "cells", "top"] + PARAMS
+OUTPUTS = ["lout", "cgrad", "sh1", "sh2", "sh3", "total"]
+
+
+def kernel_m(*refs):
+    r = Refs(INPUTS + OUTPUTS + list(SCRATCH), refs)
+    t, s = here()
+    d = 4 * t + s
+    scnt, fcnt = r.scnt[0], r.fcnt[0]
+    barrier = enter(t, s)
+    ga, gb, gc, ge = [
+        Gather(buf, r.gs.at[i], r.gq.at[i], t, s) for i, buf in enumerate((r.g1, r.g2, r.g3, r.ge))
+    ]
+    first1 = realign(r.m1, r.sh, d, 64, r.g1, d, r.ro)
+    first2 = realign(r.m2, r.sh, d, 64, r.g2, d, r.ro)
+    first3 = realign(r.m3, r.sh, d, 128, r.g3, d, r.ro)
+    r.ge[d] = jnp.concatenate([first1, first2, first3], 1).astype(BF).astype(F32)
+    pl.semaphore_wait(barrier, 10)
+    for one in (ge, ga, gb, gc):
+        one.start_z()
+        one.spread(0)
+    r.cf[s] = r.cells[:, s, :, :]
+    for one in (ge, ga):
+        one.near(0)
+        one.zin(2, 1)
+    for one in (ge, ga):
+        one.near(2, 1)
+        one.zin(3)
+    moves = [
+        send(r.cells.at[:, (s + k) % 4], r.cf.at[s], r.as1.at[k - 1], r.aq1.at[k - 1], (t, (s + k) % 4))
+        for k in (1, 2, 3)
+    ]
+    for one in (ge, ga):
+        one.near(3)
+    for one in (ge, ga):
+        one.far()
+    for one in (gb, gc):
+        one.near(0)
+        one.zin(2)
+    gb.zin(1)
+    gc.zin(1)
+    for copy in moves:
+        copy.wait_recv()
+    ge.end()
+    ga.end()
+    for one in (gb, gc):
+        one.near(2)
+        one.zin(3)
+    gb.near(1)
+    gc.near(1)
+    spread(r.g1, r.ge, 0, 64, 0, 24, put_f32(r.wide, 64))
+    split_columns(r.wide, 3, r.w1)
+    spread(r.g1, r.ge, 0, 64, 24, 32, put_bf(r.wo1, 64))
+    for k in range(3):
+        r.gains[k : k + 1, :] = r.ge[0, :, D * k : D * k + D]
+    gain1 = r.gains[0:1, :]
+
+    def norm(i, _):
+        x, _ = stats(r.cf[i].astype(F32).reshape(128, D))
+        r.a1[block(i), :] = (x * gain1).astype(BF)
+        return 0
+
+    four_blocks(norm)
+
+    def project(j, _):
+        r.qkv1[j] = nn(r.a1[...], r.w1[j]).astype(BF)
+        return 0
+
+    lax.fori_loop(0, 3, project, 0)
+    live = lax.broadcasted_iota(jnp.int32, (1, 512), 1) < scnt
+    backs = []
+    for k in (2, 1, 3, 0):
+        c = (s + k) % 4
+        if k:
+            attend_chunk(r.qkv1, c, live, r.o1c.at[k - 1])
+            backs.append(send(r.o1c.at[k - 1], r.o1.at[:, s], r.as2.at[k - 1], r.aq2.at[k - 1], (t, c)))
+        else:
+            attend_chunk(r.qkv1, c, live, r.o1.at[:, s])
+        if k == 2:
+            gb.near(3)
+            gc.near(3)
+    gb.far()
+    gb.end()
+    spread(r.g2, r.ge, 1, 64, 0, 24, put_f32(r.wide, 64))
+    split_columns(r.wide, 3, r.w2)
+    spread(r.g2, r.ge, 1, 64, 24, 32, put_bf(r.wo2, 64))
+    for copy in backs:
+        copy.wait_recv()
+    middle_forward(
+        s, r.cells, r.top, r.o1, r.wo1, r.w2, r.wo2, r.gains, scnt, fcnt, r.h1, r.h2, r.a2, r.qkv2, r.o2, r.a3, r.g
+    )
+    r.at[...] = turn(r.a3[...])
+    gc.far()
+    gc.end()
+    spread(r.g3, r.ge, 2, 128, 0, 16, put_f32(r.wide, 128))
+    split_columns(r.wide, 4, r.wup)
+
+    def put_down(i, head, last):
+        r.wdn[i // 4, pl.ds(mult((i % 4) * 128, 128), 128), :] = jnp.concatenate([head, last], 0).astype(BF)
+
+    spread(r.g3, r.ge, 2, 128, 16, 32, put_down)
+    for one in (ga, gb, gc, ge):
+        one.drain()
+    mlp(r.a3, r.at, r.g, r.h2, r.wup, r.wdn, r.h3, r.da, r.zb, r.dub, r.u, r.dz, r.wide, r.g3)
+    edge_rows(r.g3, r.ge, 2)
+
+    def reducer(n, part, i):
+        bufs = [getattr(r, k + n) for k in ("r1", "ry", "rx", "ry2", "rx2", "rz")]
+        return Reduce(part, *bufs, r.rs.at[i], r.rq.at[i], t, s)
+
+    parts = zip("abcd", (r.g1, r.g2, r.g3, r.ge))
+    sa, sb, sc, sd = [reducer(n, part, i) for i, (n, part) in enumerate(parts)]
+    sc.core()
+    layer_output(s, r.h3, r.lout, scnt, fcnt)
+    feature_grads(
+        r.wo1, r.w2, r.wo2, r.gains, fcnt, r.h1, r.h2, r.qkv2, r.g, r.da, r.b, r.b1, r.do2, r.dqkv, r.do1, r.gr,
+        r.dgain, sc.one,
+    )
+    moves2 = [
+        send(r.do1.at[:, (s + k) % 4], r.do.at[s], r.as3.at[k - 1], r.aq3.at[k - 1], (t, (s + k) % 4))
+        for k in (1, 2, 3)
+    ]
+    feature_weights(r.o1, r.a2, r.o2, r.b, r.b1, r.dqkv, r.wide, r.g2, r.dwo1)
+    edge_rows(r.g2, r.ge, 1)
+    r.do[s] = r.do1[:, s, :, :]
+    sb.core()
+    r.at[...] = turn(r.a1[...])
+    sb.one()
+    sc.two()
+    for copy in moves2:
+        copy.wait_recv()
+    live = lax.broadcasted_iota(jnp.int32, (512, 1), 0) < scnt
+
+    def heads(lo, hi):
+        def body(h, _):
+            backward_heads(h, r.qkv1, r.do, live, r.dqkv, r.kt, r.dkv)
+            return 0
+
+        lax.fori_loop(lo, hi, body, 0)
+
+    heads(0, 2)
+    sc.three()
+    sb.two()
+    heads(2, 3)
+    sb.three()
+    sc.four()
+    heads(3, 4)
+    def weights(j, _):
+        store_wide(r.wide, j, 3, nn(r.at[...], r.dqkv[j]))
+        return 0
+
+    lax.fori_loop(0, 3, weights, 0)
+
+    def narrow(i, _):
+        rows = pl.ds(mult(i * 64, 64), 64)
+        for b in range(4):
+            r.g1[i, :, 128 * b : 128 * b + 128] = r.wide[b, rows, :].astype(BF)
+        return 0
+
+    lax.fori_loop(0, 24, narrow, 0)
+
+    def copy_out(i, _):
+        r.g1[24 + i] = r.dwo1[pl.ds(mult(i * 64, 64), 64), :]
+        return 0
+
+    lax.fori_loop(0, 8, copy_out, 0)
+    edge_rows(r.g1, r.ge, 0)
+    sa.core()
+    r.da[...] = nt(r.dqkv[0], r.w1[0]) + nt(r.dqkv[1], r.w1[1]) + nt(r.dqkv[2], r.w1[2])
+    sb.four()
+    sa.one()
+
+    def norm_back(i, dg):
+        dh, part = norm_grad(r.cf[i].astype(F32).reshape(128, D), r.da[block(i), :], gain1)
+        r.dhs[i] = dh.astype(BF).reshape(4, 32, D)
+        return dg + part
+
+    dg = four_blocks(norm_back, jnp.zeros((1, D), F32))
+    homes = [
+        send(r.dhs.at[(s + k) % 4], r.dhr.at[:, s], r.as4.at[k - 1], r.aq4.at[k - 1], (t, (s + k) % 4))
+        for k in (1, 2, 3)
+    ]
+    r.ge[0] = jnp.concatenate([dg, r.dgain[1:2, :], r.dgain[2:3, :]], 1)
+    sd.core()
+    r.sums[...] = jnp.zeros((32, 128), F32)
+    for fl in (r.fl2, r.fl3):
+        fl[0:4, :] = jnp.zeros((4, 128), F32)
+    to_rows(sc.result(), r.fl3)
+    to_shard(r.fl3, 128, d, r.sh3)
+    squares(r.sh3, r.m3, r.f3, r.s3, r.sums, d, 4 * D, 2, 1, 16)
+    squares_tail(r.sh3, r.m3, r.f3, r.s3, r.sums, d, 4 * D, 2)
+    sd.one()
+    sa.two()
+    to_rows(sb.result(), r.fl2)
+    to_shard(r.fl2, 64, d, r.sh2)
+    squares(r.sh2, r.m2, r.f2, r.s2, r.sums, d, 3 * D, 1, 1, 8)
+    squares_tail(r.sh2, r.m2, r.f2, r.s2, r.sums, d, 3 * D, 1)
+    sd.two()
+    sa.three()
+    r.cgrad[:, s, :, :] = r.gr[:, s, :, :] + r.dhs[s].astype(F32)
+    for k in (1, 2, 3):
+        homes[k - 1].wait_recv()
+        f = (s + 4 - k) % 4
+        r.cgrad[:, f, :, :] = r.gr[:, f, :, :] + r.dhr[:, f, :, :].astype(F32)
+    sd.three()
+    sa.four()
+    sd.four()
+    to_rows(sa.result(), r.fl1)
+    first = sd.result()
+    for k, fl in enumerate((r.fl1, r.fl2, r.fl3)):
+        first_row(first[:, D * k : D * k + D], fl)
+    to_shard(r.fl1, 64, d, r.sh1)
+    top_shard(r.fl2, d, r.sh2)
+    top_shard(r.fl3, d, r.sh3)
+    squares(r.sh1, r.m1, r.f1, r.s1, r.sums, d, 3 * D, 0, 0, 8)
+    squares_tail(r.sh1, r.m1, r.f1, r.s1, r.sums, d, 3 * D, 0)
+    squares(r.sh2, r.m2, r.f2, r.s2, r.sums, d, 3 * D, 1, 0, 1)
+    squares(r.sh3, r.m3, r.f3, r.s3, r.sums, d, 4 * D, 2, 0, 1)
+    r.total[...], adds = sum_all(r.sums, r.ts, r.zs, r.ns, r.nq, t, s)
+    for one in (sa, sb, sc, sd):
+        one.drain()
+    for copy in moves + backs + moves2 + homes + adds:
+        copy.wait_send()
+
+
+def call_m(scnt, fcnt, cells, top, params, name="kernel_m"):
+    sds = jax.ShapeDtypeStruct
+    vm = pl.BlockSpec(memory_space=pltpu.VMEM)
+    sm = pl.BlockSpec(memory_space=pltpu.SMEM)
+    return pl.pallas_call(
+        kernel_m,
+        name=name,
+        out_shape=(
+            sds((4, 4, 32, D), BF), sds((4, 4, 32, D), F32), sds((264, 128), F32), sds((264, 128), F32),
+            sds((520, 128), F32), sds((8, 128), F32),
+        ),
+        in_specs=[sm, sm] + [vm] * 11,
+        out_specs=(vm,) * 6,
+        scratch_shapes=list(SCRATCH.values()),
+        compiler_params=pltpu.CompilerParams(collective_id=1, has_side_effects=True, vmem_limit_bytes=63 << 20),
+    )(scnt, fcnt, cells, top, *params)
+
+
+def local(x):
+    return jnp.transpose(x.reshape(4, 32, 4, D), (0, 2, 1, 3))
+
+
+def globe(x):
+    return jnp.transpose(x, (0, 2, 1, 3)).reshape(1, 128, 4, D)
+
+
+def fast_device(cells, out_grad, scnt, fcnt, b1, f1, s1, b2, f2, s2, b3, f3, s3):
+    params = (b1, f1, s1, b2, f2, s2, b3, f3, s3)
+    out, cgrad, sh1, sh2, sh3, total = call_m(scnt, fcnt, local(cells), local(out_grad), params)
+    outs = call_e(total, (sh1, sh2, sh3), params)
+    return (globe(out), globe(cgrad), *outs)
+
+
+def step(*args):
+    cells = args[0]
+    fits = lax.axis_size("task") == 8 and lax.axis_size("samp") == 4 and cells.shape == (1, 128, 4, D)
+    return fast_device(*args) if fits else on_device(*args)
+
+
 def solution(mesh):
     placed = (
         P("task", "samp", None, None),
@@ -377,7 +1422,7 @@
         P(("task", "samp")),
     )
     return jax.shard_map(
-        on_device,
+        step,
         mesh=mesh,
         in_specs=placed,
         out_specs=(

time: 1000 us -> 165 us (0.17)
  waiting for transfers between devices: 568 us -> 0 us
  local copies, waits for them, and re-layouts: 196 us -> 7.24 us
  Pallas kernels: 0 us -> 155 us
  matrix products: 112 us -> 0 us
  other arithmetic: 60.8 us -> 0 us
  blocking collectives: 39.3 us -> 0 us
  between operations: 16.3 us -> 2.16 us
    unnamed x5 -> x0, waiting for transfers between devices: 447 us -> none
    pallas_call x0 -> x2, Pallas kernels: none -> 155 us  [the longest x1 152 us: call_m(): pl.pallas_call(kernel_m, name=name, out_shape=(sds((4, 4, 32, D), BF), sd...]
    dot_general x37 -> x0, matrix products: 106 us -> none  [the longest x6 17.4 us: contract_rows(): lax.dot_general(left, right, (((0,), (0,)), ((), ())), preferred_element_...]
    while x4 -> x0, waiting for transfers between devices: 80.1 us -> none
    reshape x17 -> x0, local copies, waits for them, and re-layouts: 46.8 us -> none  [the longest x6 22.5 us: unpack(): w_in = flat_params[D:D + D * width_in].reshape(D, width_in)]
    while x13 -> x0, local copies, waits for them, and re-layouts: 41.1 us -> none
    all_gather x1 -> x0, waiting for transfers between devices: 40.5 us -> none  [on_device(): pairs_all = lax.all_gather(pairs_local, 'samp', axis=0, tiled=True)]
    psum x1 -> x0, blocking collectives: 39.3 us -> none  [on_device(): lax.psum(jnp.concatenate([sample_state[4], feature_state[4], mlp_state[4]...]
  transfers between devices with their start and end apart: 5 -> 0, of which waited for: 5 -> 0; matrix products, arithmetic and copies ran while one was open for 6% -> 0% of each run, Pallas kernels for 0% -> 0%
where the time goes in v1:
time: 165 us
  Pallas kernels  155 us (94%)
  local copies, waits for them, and re-layouts  7.24 us (4%)
  between operations  2.16 us (1%)
    pallas_call x1, Pallas kernels, call_m(): pl.pallas_call(kernel_m, name=name, out_shape=(sds((4, 4, 32, D), BF), sd...  152 us
    unnamed x31, local copies, waits for them, and re-layouts  3.57 us

profile of v1, /device:TPU:0, one launch (start us, length us, event | category | flops | bytes accessed | tf_op | source)
XLA Modules:
  0.0 164.8 jit_solution(4599717614296713795)
XLA Ops:
  1.9 2.4 %copy_bitcast_fusion = (bf16[4,4,32,512]{3,2,1,0:T(8,128)(2,1)}, bf16[4,4,32,512]{3,2,1,0:T(8,128)(2,1)}) fusion(bf16[4,32,4,512]{3,2,1,0:T(4,128)(2,1)} %bitcast.14, bf16[4,32,4,512]{3,2,1,0:T(4,128)(2,1)} %bitcast.15), kind=kLoop, calls=%fused_computation | loop fusion | bytes 2097152 | tf_op jit(solution)/shard_map/transpose | solution.py:1388
  4.4 152.5 %kernel_m.1 = (bf16[4,4,32,512]{3,2,1,0:T(8,128)(2,1)}, f32[4,4,32,512]{3,2,1,0:T(8,128)}, f32[264,128]{1,0:T(8,128)}, f32[264,128]{1,0:T(8,128)}, f32[520,128]{1,0:T(8,128)}, /*index=5*/f32[8,128]{1,0:T(8,128)}) custom-call(s32[1]{0:T(128)S(6)} %copy.47.refs_0_, s32[1]{0:T(128)S(6)} %copy.48.refs_1_, bf16[4,4,32,512]{3,2,1,0:T(8,128)(2,1)} %get-tuple-element.99.refs_2_, ...), custom_call_target="tpu_custom_call" | custom-call | tf_op jit(solution)/shard_map/kernel_m/pallas_call | solution.py:1373
  156.9 0.0 copy-start.13
  156.9 1.2 copy.36
  158.0 1.2 copy.38
  159.2 0.0 copy-done.13
  159.2 0.1 copy.37
  159.3 0.0 copy-start
  159.4 0.0 copy-start.1
  159.4 0.0 copy-start.2
  159.4 0.0 copy-start.3
  159.4 0.0 copy-start.4
  159.4 0.0 copy-start.5
  159.4 0.0 copy-start.6
  159.4 0.0 copy-start.7
  159.4 0.0 copy-start.8
  159.5 0.0 copy-start.9
  159.5 0.0 copy-start.10
  159.5 0.0 copy-start.12
  159.5 1.6 copy.39
  161.1 0.0 copy-done.11
  161.1 0.0 copy-done.1
  161.2 2.9 %kernel_e.1 = (f32[32784]{0:T(1024)}, f32[32784]{0:T(1024)}, f32[32784]{0:T(1024)}, f32[32784]{0:T(1024)}, bf16[32784]{0:T(1024)(128)(2,1)}, /*index=5*/f32[3278...) custom-call(f32[8,128]{1,0:T(8,128)S(1)} %copy-done.12, ...), custom_call_target="tpu_custom_call" | custom-call | tf_op jit(solution)/shard_map/kernel_e/pallas_call | solution.py:708
  164.2 0.6 copy.40
  (12 shorter events, 0.0 us)
Async XLA Ops:
  156.9 2.4 %copy-start.13 = (f32[4,4,32,512]{3,2,1,0:T(8,128)S(1)}, f32[4,4,32,512]{3,2,1,0:T(8,128)}, u32[]{:S(2)}) copy-start(f32[4,4,32,512]{3,2,1,0:T(8,128)} %get-tuple-element.41) | copy-start | bytes 3145732
  159.2 1.9 %copy-start.11 = (f32[264,128]{1,0:T(8,128)S(1)}, f32[264,128]{1,0:T(8,128)}, u32[]{:S(2)}) copy-start(f32[264,128]{1,0:T(8,128)} %get-tuple-element.44.sh2) | copy-start | bytes 405508
  159.3 1.8 %copy-start = (f32[65552]{0:T(1024)S(1)}, f32[65552]{0:T(1024)}, u32[]{:S(2)}) copy-start(f32[65552]{0:T(1024)} %m3.1) | copy-start | bytes 786628
  159.4 1.8 %copy-start.1 = (f32[65552]{0:T(1024)S(1)}, f32[65552]{0:T(1024)}, u32[]{:S(2)}) copy-start(f32[65552]{0:T(1024)} %f3.1) | copy-start | bytes 786628
  159.4 1.8 %copy-start.2 = (f32[65552]{0:T(1024)S(1)}, f32[65552]{0:T(1024)}, u32[]{:S(2)}) copy-start(f32[65552]{0:T(1024)} %s3.1) | copy-start | bytes 786628
  159.4 1.8 %copy-start.3 = (f32[32784]{0:T(1024)S(1)}, f32[32784]{0:T(1024)}, u32[]{:S(2)}) copy-start(f32[32784]{0:T(1024)} %m1.1) | copy-start | bytes 393412
  159.4 1.8 %copy-start.4 = (f32[32784]{0:T(1024)S(1)}, f32[32784]{0:T(1024)}, u32[]{:S(2)}) copy-start(f32[32784]{0:T(1024)} %f1.1) | copy-start | bytes 393412
  159.4 1.8 %copy-start.5 = (f32[32784]{0:T(1024)S(1)}, f32[32784]{0:T(1024)}, u32[]{:S(2)}) copy-start(f32[32784]{0:T(1024)} %s1_.1) | copy-start | bytes 393412
  159.4 1.8 %copy-start.6 = (f32[32784]{0:T(1024)S(1)}, f32[32784]{0:T(1024)}, u32[]{:S(2)}) copy-start(f32[32784]{0:T(1024)} %m2.1) | copy-start | bytes 393412
  159.4 1.8 %copy-start.7 = (f32[32784]{0:T(1024)S(1)}, f32[32784]{0:T(1024)}, u32[]{:S(2)}) copy-start(f32[32784]{0:T(1024)} %f2.1) | copy-start | bytes 393412
  159.4 1.8 %copy-start.8 = (f32[32784]{0:T(1024)S(1)}, f32[32784]{0:T(1024)}, u32[]{:S(2)}) copy-start(f32[32784]{0:T(1024)} %s2_.1) | copy-start | bytes 393412
  159.5 1.8 %copy-start.9 = (f32[520,128]{1,0:T(8,128)S(1)}, f32[520,128]{1,0:T(8,128)}, u32[]{:S(2)}) copy-start(f32[520,128]{1,0:T(8,128)} %get-tuple-element.45.sh3) | copy-start | bytes 798724
  159.5 1.8 %copy-start.10 = (f32[264,128]{1,0:T(8,128)S(1)}, f32[264,128]{1,0:T(8,128)}, u32[]{:S(2)}) copy-start(f32[264,128]{1,0:T(8,128)} %get-tuple-element.43.sh1) | copy-start | bytes 405508
  159.5 1.8 %copy-start.12 = (f32[8,128]{1,0:T(8,128)S(1)}, f32[8,128]{1,0:T(8,128)}, u32[]{:S(2)}) copy-start(f32[8,128]{1,0:T(8,128)} %get-tuple-element.42.total) | copy-start | bytes 12292

commit v2 on v1

--- a/solution.py
+++ b/solution.py
@@ -474,7 +474,7 @@
             copy.wait_send()
 
 
-def realign(m_ref, sh_ref, d, rows, out_ref, out_at, roll_to):
+def realign(m_ref, sh_ref, d, rows, out_ref, out_at, roll_to, split=False):
     whole = 4 * rows
     total = whole + 8
     q, p = d // 8, d % 8
@@ -489,8 +489,25 @@
     sh_ref[0:8, :] = jnp.zeros((8, 128), F32)
     sh_ref[8 : 8 + total, :] = jnp.where(lane < 16 * p, roll_to[7 : 7 + total, :], rolled)
     firsts = []
+
+    def straight():
+        for b in range(4):
+            cols = slice(128 * b, 128 * b + 128)
+            out_ref[out_at, 0:rows, cols] = sh_ref[pl.ds(12 - q + b, rows, stride=4), :].astype(BF)
+
+    def by_piece():
+        for b in range(4):
+            cols = slice(128 * b, 128 * b + 128)
+            for j in range(4):
+                piece = sh_ref[pl.ds(12 - q + b + 4 * j, rows // 4, stride=16), :]
+                out_ref[out_at, rows // 4 * j : rows // 4 * (j + 1), cols] = piece.astype(BF)
+
+    if split:
+        pl.when(d < 16)(by_piece)
+        pl.when(d >= 16)(straight)
+    else:
+        straight()
     for b in range(4):
-        out_ref[out_at, 0:rows, 128 * b : 128 * b + 128] = sh_ref[pl.ds(12 - q + b, rows, stride=4), :].astype(BF)
         firsts.append(sh_ref[pl.ds(8 - q + b, 1), :])
     return jnp.concatenate(firsts, 1)
 
@@ -684,21 +701,30 @@
     return (zs[0] + zs[1]) + (zs[2] + zs[3]), plane + last
 
 
+def by_sample(x, out):
+    for g in range(4):
+        out[32 * g : 32 * g + 32, :, :] = jnp.transpose(x[g].astype(F32), (1, 0, 2)).astype(out.dtype)
+
+
 def kernel_e(
-    total, sh1, sh2, sh3, m1, f1, s1, m2, f2, s2, m3, f3, s3,
-    g1, fo1, so1, mo1, wo1, g2, fo2, so2, mo2, wo2, g3, fo3, so3, mo3, wo3, pairs,
+    total, sh1, sh2, sh3, m1, f1, s1, m2, f2, s2, m3, f3, s3, lout, cgrad,
+    g1, fo1, so1, mo1, wo1, g2, fo2, so2, mo2, wo2, g3, fo3, so3, mo3, wo3, pairs, layer, grad,
 ):
     t, s = here()
     d = 4 * t + s
-    norm = jnp.sqrt(jnp.sum(jnp.where(diagonal(32), total[0:1, :], 0.0), 1, keepdims=True))
-    pairs[...] = jnp.concatenate([norm[0:9], norm[16:25]], 1)
+    norms = jnp.sqrt(total[0:1, :])
+    pairs[0:1, :] = norms[:, 0:9]
+    pairs[1:2, :] = pltpu.roll(norms, 112, 1)[:, 0:9]
+    norm = jnp.sum(jnp.where(diagonal(32), norms, 0.0), 1, keepdims=True)
     ratio = norm[0:9] / (norm[16:25] + 1e-6)
+    by_sample(lout, layer)
+    by_sample(cgrad, grad)
     update(sh1, m1, f1, s1, g1, fo1, so1, mo1, wo1, ratio, d, 3 * D, 0)
     update(sh2, m2, f2, s2, g2, fo2, so2, mo2, wo2, ratio, d, 3 * D, 1)
     update(sh3, m3, f3, s3, g3, fo3, so3, mo3, wo3, ratio, d, 4 * D, 2)
 
 
-def call_e(total, shards, args):
+def call_e(total, shards, args, lout, cgrad):
     sds = jax.ShapeDtypeStruct
     vm = pl.BlockSpec(memory_space=pltpu.VMEM)
     shapes = []
@@ -708,11 +734,11 @@
     return pl.pallas_call(
         kernel_e,
         name="kernel_e",
-        out_shape=(*shapes, sds((9, 2), F32)),
-        in_specs=[vm] * 13,
-        out_specs=(vm,) * 16,
-        compiler_params=pltpu.CompilerParams(vmem_limit_bytes=40 << 20),
-    )(total, *shards, *args)
+        out_shape=(*shapes, sds((2, 9), F32), sds((128, 4, D), BF), sds((128, 4, D), F32)),
+        in_specs=[vm] * 15,
+        out_specs=(vm,) * 18,
+        compiler_params=pltpu.CompilerParams(vmem_limit_bytes=63 << 20),
+    )(total, *shards, *args, lout, cgrad)
 
 
 def backward_heads(h, qkv, do, live, dqkv, kt, dkv):
@@ -848,7 +874,7 @@
         wide[b, pl.ds(j, value.shape[0], stride=ways), :] = value[:, 128 * b : 128 * b + 128]
 
 
-def mlp(a3, a3t, g, h2, wup, wdn, h3, da, zb, dub, u, dz, wide, p3):
+def mlp(a3, a3t, g, h2, wup, wdn, h3, da, zb, dub, u, dz, p3):
     h3[...] = h2[...]
     da[...] = jnp.zeros((512, D), F32)
 
@@ -868,17 +894,18 @@
         lax.fori_loop(0, 8, act, 0)
         h3[...] += nn(zb[...], wdn[j])
         da[...] += nt(dub[...], wup[j])
-        store_wide(wide, j, 4, nn(a3t[...], dub[...]))
+        up = nn(a3t[...], dub[...]).astype(BF)
+        for i in range(16):
+            p3[i, pl.ds(mult(32 * j, 32), 32), :] = up[32 * i : 32 * i + 32]
         dw = nn(turn(zb[...]), g[...]).astype(BF)
         for i in range(4):
             p3[16 + 4 * j + i] = dw[128 * i : 128 * i + 128]
         return 0
 
     lax.fori_loop(0, 4, body, 0)
-    narrow_to(wide, p3, 16, 128)
-
-
-def middle_forward(s, cells, top, o1, wo1, w2, wo2, gains, scnt, fcnt, h1, h2, a2, qkv, o2, a3, g):
+
+
+def middle_forward(s, cells, top, o1, wo1, w2, wo2, gains, scnt, fcnt, h1, h2, a2, qkv, o2, a3, g, hook):
     gain2, gain3 = gains[1:2, :], gains[2:3, :]
     h1[...] = nn(o1[...].reshape(512, D), wo1[...])
 
@@ -900,6 +927,7 @@
         return 0
 
     lax.fori_loop(0, 3, project, 0)
+    hook()
     feature_forward(qkv, o2, fcnt)
     h2[...] = h1[...] + nn(o2[...], wo2[...])
 
@@ -922,7 +950,7 @@
     four_blocks(last)
 
 
-def feature_grads(wo1, w2, wo2, gains, fcnt, h1, h2, qkv, g, da, b2, b1, do, dqkv, do1, gr, dgain, hook):
+def feature_grads(wo1, w2, wo2, gains, fcnt, h1, h2, qkv, g, da, b2, b1, do, dqkv, do1, gr, dgain):
     gain2, gain3 = gains[1:2, :], gains[2:3, :]
 
     def third(r, dg):
@@ -936,7 +964,6 @@
     dg3 = four_blocks(third, jnp.zeros((1, D), F32))
     do[...] = nt(b2[...], wo2[...]).astype(BF)
     feature_backward(qkv, do, dqkv, fcnt)
-    hook()
     da[...] = nt(dqkv[0], w2[0]) + nt(dqkv[1], w2[1]) + nt(dqkv[2], w2[2])
 
     def fourth(r, dg):
@@ -967,11 +994,16 @@
 
 
 class Reduce:
-    def __init__(self, part, r1, ry, rx, ry2, rx2, rz, ssem, rsem, t, s):
+    def __init__(self, part, r1, ry, rx, ry2, rx2, rz, ssem, rsem, t, s, chunk=None):
         self.part, self.r1 = part, r1
         self.ry, self.rx, self.ry2, self.rx2, self.rz = ry, rx, ry2, rx2, rz
-        half = part.shape[2] // 2
-        self.ha, self.hb, self.all = pl.ds(0, half), pl.ds(half, half), pl.ds(0, 2 * half)
+        rows, half = part.shape[1], part.shape[2] // 2
+        if chunk is None:
+            every = pl.ds(0, rows)
+            self.ha, self.hb, self.all = [(every, pl.ds(o, n)) for o, n in ((0, half), (half, half), (0, 2 * half))]
+        else:
+            cols, half = pl.ds(128 * chunk, 128), rows // 2
+            self.ha, self.hb, self.all = [(pl.ds(o, n), cols) for o, n in ((0, half), (half, half), (0, rows))]
         self.ssem, self.rsem, self.t, self.s = ssem, rsem, t, s
         self.copies = []
 
@@ -984,21 +1016,22 @@
     def xor(self, e):
         return jnp.bitwise_xor(self.t, e)
 
-    def group(self, e, cols):
-        return self.part.at[pl.ds(4 * self.xor(2 * e), 4), :, cols]
+    def group(self, e, box, t=None):
+        t = self.t if t is None else t
+        return self.part.at[pl.ds(4 * jnp.bitwise_xor(t, 2 * e), 4), *box]
 
     def core(self):
         tc = self.xor(1)
         self.c = [
-            self.go(self.part.at[pl.ds(4 * jnp.bitwise_xor(tc, 2 * e), 4)], self.r1.at[e], (tc, self.s))
+            self.go(self.group(e, self.all, tc), self.r1.at[e], (tc, self.s))
             for e in (2, 3, 1, 0)
         ]
 
-    def add(self, e, cols, got):
+    def add(self, e, box, got):
         base = 4 * self.xor(2 * e)
         for j in range(4):
-            own = self.part[base + j, :, cols].astype(F32)
-            self.part[base + j, :, cols] = (own + got[j].astype(F32)).astype(self.part.dtype)
+            own = self.part[base + j, *box].astype(F32)
+            self.part[base + j, *box] = (own + got[j].astype(F32)).astype(self.part.dtype)
 
     def one(self):
         ty, tx, s = self.xor(4), self.xor(2), self.s
@@ -1034,19 +1067,19 @@
     def z_send(self, slot, into):
         t, s = self.t, self.s
         to = jnp.bitwise_xor(s, 2 if into == 2 else 1)
-        return self.go(self.part.at[4 * t + jnp.bitwise_xor(s, slot)], self.rz.at[into], (t, to))
+        return self.go(self.part.at[4 * t + jnp.bitwise_xor(s, slot), *self.all], self.rz.at[into], (t, to))
 
     def four(self):
         self.z[1].wait_recv()
         mine = 4 * self.t + jnp.bitwise_xor(self.s, 2)
-        own = self.part[mine, :, :].astype(F32)
-        self.part[mine, :, :] = (own + self.rz[1, :, :].astype(F32)).astype(self.part.dtype)
+        own = self.part[mine, *self.all].astype(F32)
+        self.part[mine, *self.all] = (own + self.rz[1, :, :].astype(F32)).astype(self.part.dtype)
         self.z.append(self.z_send(2, 2))
 
     def result(self):
         self.z[0].wait_recv()
         self.z[2].wait_recv()
-        own = self.part[4 * self.t + self.s, :, :].astype(F32)
+        own = self.part[4 * self.t + self.s, *self.all].astype(F32)
         return own + self.rz[0, :, :].astype(F32) + self.rz[2, :, :].astype(F32)
 
     def drain(self):
@@ -1054,15 +1087,20 @@
             copy.wait_send()
 
 
-def edge_rows(part, edges, kind):
+def edge_rows(part, edges, kind, lo=0, size=D):
     rows = part.shape[1]
 
     def body(i, _):
-        row = part[i - 1, rows - 16 : rows, :].astype(F32)[15:16, :]
-        edges[i, :, D * kind : D * kind + D] = row
+        row = part[i - 1, rows - 16 : rows, lo : lo + size].astype(F32)[15:16, :]
+        edges[i, :, D * kind + lo : D * kind + lo + size] = row
         return 0
 
     lax.fori_loop(1, 32, body, 0)
+
+
+def by_feature(x, out):
+    for g in range(4):
+        out[g] = jnp.transpose(x[32 * g : 32 * g + 32, :, :].astype(F32), (1, 0, 2)).astype(BF)
 
 
 def to_rows(main, fl):
@@ -1112,6 +1150,12 @@
         pltpu.VMEM((2, 4, rows, half), kind), pltpu.VMEM((4, rows, half), kind), pltpu.VMEM((4, rows, half), kind),
         pltpu.VMEM((3, rows, width), kind),
     ]
+
+
+def chunk_scratch(rows):
+    half = rows // 2
+    shapes = [(4, 4, rows), (2, 4, half), (2, 4, half), (4, half), (4, half), (3, rows)]
+    return [pltpu.VMEM((*shape, 128), BF) for shape in shapes]
 
 
 PARAMS = ["m1", "f1", "s1", "m2", "f2", "s2", "m3", "f3", "s3"]
@@ -1126,22 +1170,22 @@
     "wide": pltpu.VMEM((4, 4 * D, 128), F32), "sh": pltpu.VMEM((536, 128), F32), "ro": pltpu.VMEM((536, 128), F32),
     "w1": THREE, "wo1": NARROW, "w2": THREE, "wo2": NARROW, "wup": FOUR, "wdn": FOUR,
     "gains": pltpu.VMEM((8, D), F32), "dgain": pltpu.VMEM((8, D), F32),
-    "cf": TILE, "a1": NARROW, "qkv1": THREE, "o1c": pltpu.VMEM((3, 4, 32, D), BF), "o1": TILE,
+    "cells": TILE, "top": TILE, "cf": TILE, "a1": NARROW, "qkv1": THREE, "o1c": pltpu.VMEM((3, 4, 32, D), BF), "o1": TILE,
     "h1": WIDE, "h2": WIDE, "a2": NARROW, "qkv2": THREE, "o2": NARROW, "a3": NARROW, "at": NARROW, "g": NARROW,
     "h3": WIDE, "da": WIDE, "zb": NARROW, "dub": NARROW, "u": WIDE, "dz": NARROW, "b": NARROW, "b1": NARROW, "do2": NARROW,
     "dqkv": THREE, "gr": pltpu.VMEM((4, 4, 32, D), F32), "do1": TILE, "do": TILE, "dwo1": NARROW,
     "kt": pltpu.VMEM((128, D), BF), "dkv": pltpu.VMEM((2, D, 128), F32), "dhs": TILE, "dhr": TILE,
-    **dict(zip(reduce_names("a"), reduce_scratch(64))),
+    **{k: v for h in range(4) for k, v in zip(reduce_names(f"a{h}"), chunk_scratch(64))},
     **dict(zip(reduce_names("b"), reduce_scratch(64))),
     **dict(zip(reduce_names("c"), reduce_scratch(128))),
     **dict(zip(reduce_names("d"), reduce_scratch(1, 3 * D, F32))),
     "fl1": pltpu.VMEM((272, 128), F32), "fl2": pltpu.VMEM((272, 128), F32), "fl3": pltpu.VMEM((528, 128), F32),
     "sums": pltpu.VMEM((32, 128), F32), "ts": pltpu.VMEM((8, 8, 128), F32), "zs": pltpu.VMEM((4, 8, 128), F32),
-    "gs": DMA((4, 32)), "gq": DMA((4, 32)), "rs": DMA((4, 16)), "rq": DMA((4, 16)),
+    "gs": DMA((4, 32)), "gq": DMA((4, 32)), "rs": DMA((7, 16)), "rq": DMA((7, 16)),
     "as1": DMA((3,)), "aq1": DMA((3,)), "as2": DMA((3,)), "aq2": DMA((3,)),
     "as3": DMA((3,)), "aq3": DMA((3,)), "as4": DMA((3,)), "aq4": DMA((3,)), "ns": DMA((10,)), "nq": DMA((10,)),
 }
-INPUTS = ["scnt", "fcnt", "cells", "top"] + PARAMS
+INPUTS = ["scnt", "fcnt", "cells_in", "top_in"] + PARAMS
 OUTPUTS = ["lout", "cgrad", "sh1", "sh2", "sh3", "total"]
 
 
@@ -1156,12 +1200,13 @@
     ]
     first1 = realign(r.m1, r.sh, d, 64, r.g1, d, r.ro)
     first2 = realign(r.m2, r.sh, d, 64, r.g2, d, r.ro)
-    first3 = realign(r.m3, r.sh, d, 128, r.g3, d, r.ro)
+    first3 = realign(r.m3, r.sh, d, 128, r.g3, d, r.ro, True)
     r.ge[d] = jnp.concatenate([first1, first2, first3], 1).astype(BF).astype(F32)
     pl.semaphore_wait(barrier, 10)
     for one in (ge, ga, gb, gc):
         one.start_z()
         one.spread(0)
+    by_feature(r.cells_in, r.cells)
     r.cf[s] = r.cells[:, s, :, :]
     for one in (ge, ga):
         one.near(0)
@@ -1175,22 +1220,21 @@
     ]
     for one in (ge, ga):
         one.near(3)
+    by_feature(r.top_in, r.top)
     for one in (ge, ga):
         one.far()
     for one in (gb, gc):
         one.near(0)
         one.zin(2)
     gb.zin(1)
-    gc.zin(1)
     for copy in moves:
         copy.wait_recv()
     ge.end()
     ga.end()
-    for one in (gb, gc):
-        one.near(2)
-        one.zin(3)
+    gb.near(2)
+    gb.zin(3)
+    gc.zin(1)
     gb.near(1)
-    gc.near(1)
     spread(r.g1, r.ge, 0, 64, 0, 24, put_f32(r.wide, 64))
     split_columns(r.wide, 3, r.w1)
     spread(r.g1, r.ge, 0, 64, 24, 32, put_bf(r.wo1, 64))
@@ -1212,6 +1256,9 @@
     lax.fori_loop(0, 3, project, 0)
     live = lax.broadcasted_iota(jnp.int32, (1, 512), 1) < scnt
     backs = []
+    gb.near(3)
+    gc.near(2)
+    gc.zin(3)
     for k in (2, 1, 3, 0):
         c = (s + k) % 4
         if k:
@@ -1219,24 +1266,29 @@
             backs.append(send(r.o1c.at[k - 1], r.o1.at[:, s], r.as2.at[k - 1], r.aq2.at[k - 1], (t, c)))
         else:
             attend_chunk(r.qkv1, c, live, r.o1.at[:, s])
-        if k == 2:
-            gb.near(3)
-            gc.near(3)
-    gb.far()
+        if k == 1:
+            gb.far()
+            gc.near(1)
     gb.end()
     spread(r.g2, r.ge, 1, 64, 0, 24, put_f32(r.wide, 64))
     split_columns(r.wide, 3, r.w2)
     spread(r.g2, r.ge, 1, 64, 24, 32, put_bf(r.wo2, 64))
+    gc.near(3)
     for copy in backs:
         copy.wait_recv()
     middle_forward(
-        s, r.cells, r.top, r.o1, r.wo1, r.w2, r.wo2, r.gains, scnt, fcnt, r.h1, r.h2, r.a2, r.qkv2, r.o2, r.a3, r.g
+        s, r.cells, r.top, r.o1, r.wo1, r.w2, r.wo2, r.gains, scnt, fcnt, r.h1, r.h2, r.a2, r.qkv2, r.o2, r.a3, r.g,
+        gc.far,
     )
     r.at[...] = turn(r.a3[...])
-    gc.far()
     gc.end()
-    spread(r.g3, r.ge, 2, 128, 0, 16, put_f32(r.wide, 128))
-    split_columns(r.wide, 4, r.wup)
+
+    def put_up(i, head, last):
+        block = jnp.concatenate([head, last], 0).astype(BF)
+        for j in range(4):
+            r.wup[j, pl.ds(mult(i * 32, 32), 32), :] = block[32 * j : 32 * j + 32]
+
+    spread(r.g3, r.ge, 2, 128, 0, 16, put_up)
 
     def put_down(i, head, last):
         r.wdn[i // 4, pl.ds(mult((i % 4) * 128, 128), 128), :] = jnp.concatenate([head, last], 0).astype(BF)
@@ -1244,74 +1296,69 @@
     spread(r.g3, r.ge, 2, 128, 16, 32, put_down)
     for one in (ga, gb, gc, ge):
         one.drain()
-    mlp(r.a3, r.at, r.g, r.h2, r.wup, r.wdn, r.h3, r.da, r.zb, r.dub, r.u, r.dz, r.wide, r.g3)
+    mlp(r.a3, r.at, r.g, r.h2, r.wup, r.wdn, r.h3, r.da, r.zb, r.dub, r.u, r.dz, r.g3)
     edge_rows(r.g3, r.ge, 2)
 
-    def reducer(n, part, i):
-        bufs = [getattr(r, k + n) for k in ("r1", "ry", "rx", "ry2", "rx2", "rz")]
-        return Reduce(part, *bufs, r.rs.at[i], r.rq.at[i], t, s)
-
-    parts = zip("abcd", (r.g1, r.g2, r.g3, r.ge))
-    sa, sb, sc, sd = [reducer(n, part, i) for i, (n, part) in enumerate(parts)]
+    def reducer(n, part, i, chunk=None):
+        bufs = [getattr(r, k) for k in reduce_names(n)]
+        return Reduce(part, *bufs, r.rs.at[i], r.rq.at[i], t, s, chunk)
+
+    sb, sc, sd = reducer("b", r.g2, 0), reducer("c", r.g3, 1), reducer("d", r.ge, 2)
+    sa = [reducer(f"a{h}", r.g1, 3 + h, h) for h in range(4)]
     sc.core()
     layer_output(s, r.h3, r.lout, scnt, fcnt)
     feature_grads(
         r.wo1, r.w2, r.wo2, r.gains, fcnt, r.h1, r.h2, r.qkv2, r.g, r.da, r.b, r.b1, r.do2, r.dqkv, r.do1, r.gr,
-        r.dgain, sc.one,
+        r.dgain,
     )
     moves2 = [
         send(r.do1.at[:, (s + k) % 4], r.do.at[s], r.as3.at[k - 1], r.aq3.at[k - 1], (t, (s + k) % 4))
         for k in (1, 2, 3)
     ]
+    sc.one()
     feature_weights(r.o1, r.a2, r.o2, r.b, r.b1, r.dqkv, r.wide, r.g2, r.dwo1)
     edge_rows(r.g2, r.ge, 1)
     r.do[s] = r.do1[:, s, :, :]
     sb.core()
     r.at[...] = turn(r.a1[...])
-    sb.one()
-    sc.two()
     for copy in moves2:
         copy.wait_recv()
     live = lax.broadcasted_iota(jnp.int32, (512, 1), 0) < scnt
 
-    def heads(lo, hi):
-        def body(h, _):
-            backward_heads(h, r.qkv1, r.do, live, r.dqkv, r.kt, r.dkv)
-            return 0
-
-        lax.fori_loop(lo, hi, body, 0)
-
-    heads(0, 2)
-    sc.three()
-    sb.two()
-    heads(2, 3)
-    sb.three()
-    sc.four()
-    heads(3, 4)
-    def weights(j, _):
-        store_wide(r.wide, j, 3, nn(r.at[...], r.dqkv[j]))
-        return 0
-
-    lax.fori_loop(0, 3, weights, 0)
-
-    def narrow(i, _):
-        rows = pl.ds(mult(i * 64, 64), 64)
-        for b in range(4):
-            r.g1[i, :, 128 * b : 128 * b + 128] = r.wide[b, rows, :].astype(BF)
-        return 0
-
-    lax.fori_loop(0, 24, narrow, 0)
-
     def copy_out(i, _):
         r.g1[24 + i] = r.dwo1[pl.ds(mult(i * 64, 64), 64), :]
         return 0
 
     lax.fori_loop(0, 8, copy_out, 0)
-    edge_rows(r.g1, r.ge, 0)
-    sa.core()
+
+    def heads(h):
+        backward_heads(h, r.qkv1, r.do, live, r.dqkv, r.kt, r.dkv)
+        cols = slice(128 * h, 128 * h + 128)
+        for j in range(3):
+            r.wide[h, pl.ds(j, D, stride=3), :] = nn(r.at[...], r.dqkv[j, :, cols])
+
+        def narrow(i, _):
+            r.g1[i, :, cols] = r.wide[h, pl.ds(mult(i * 64, 64), 64), :].astype(BF)
+            return 0
+
+        lax.fori_loop(0, 24, narrow, 0)
+        edge_rows(r.g1, r.ge, 0, 128 * h, 128)
+        sa[h].core()
+
+    heads(0)
+    sc.two()
+    sb.one()
+    heads(1)
+    sa[0].one()
+    heads(2)
+    sc.three()
+    sa[1].one()
+    sa[0].two()
+    heads(3)
     r.da[...] = nt(r.dqkv[0], r.w1[0]) + nt(r.dqkv[1], r.w1[1]) + nt(r.dqkv[2], r.w1[2])
-    sb.four()
-    sa.one()
+    sb.two()
+    sa[2].one()
+    sa[1].two()
 
     def norm_back(i, dg):
         dh, part = norm_grad(r.cf[i].astype(F32).reshape(128, D), r.da[block(i), :], gain1)
@@ -1319,36 +1366,55 @@
         return dg + part
 
     dg = four_blocks(norm_back, jnp.zeros((1, D), F32))
+    r.ge[0] = jnp.concatenate([dg, r.dgain[1:2, :], r.dgain[2:3, :]], 1)
+    sd.core()
+    sa[3].one()
+    sc.four()
+    sb.three()
+    sa[0].three()
+    sa[2].two()
+    sa[1].three()
+    sd.one()
+    sa[0].four()
+    sa[3].two()
+    sa[2].three()
+    sa[1].four()
+    sd.two()
+    sb.four()
+    sa[3].three()
+    sa[2].four()
+    sd.three()
     homes = [
         send(r.dhs.at[(s + k) % 4], r.dhr.at[:, s], r.as4.at[k - 1], r.aq4.at[k - 1], (t, (s + k) % 4))
         for k in (1, 2, 3)
     ]
-    r.ge[0] = jnp.concatenate([dg, r.dgain[1:2, :], r.dgain[2:3, :]], 1)
-    sd.core()
     r.sums[...] = jnp.zeros((32, 128), F32)
     for fl in (r.fl2, r.fl3):
         fl[0:4, :] = jnp.zeros((4, 128), F32)
-    to_rows(sc.result(), r.fl3)
+    main = sc.result()
+
+    @pl.when(d < 16)
+    def _():
+        for j in range(4):
+            for b in range(4):
+                piece = main[32 * j : 32 * j + 32, 128 * b : 128 * b + 128]
+                r.fl3[pl.ds(4 + b + 4 * j, 32, stride=16), :] = piece
+
+    @pl.when(d >= 16)
+    def _():
+        to_rows(main, r.fl3)
+
     to_shard(r.fl3, 128, d, r.sh3)
     squares(r.sh3, r.m3, r.f3, r.s3, r.sums, d, 4 * D, 2, 1, 16)
     squares_tail(r.sh3, r.m3, r.f3, r.s3, r.sums, d, 4 * D, 2)
-    sd.one()
-    sa.two()
+    sa[3].four()
+    sd.four()
     to_rows(sb.result(), r.fl2)
     to_shard(r.fl2, 64, d, r.sh2)
     squares(r.sh2, r.m2, r.f2, r.s2, r.sums, d, 3 * D, 1, 1, 8)
     squares_tail(r.sh2, r.m2, r.f2, r.s2, r.sums, d, 3 * D, 1)
-    sd.two()
-    sa.three()
-    r.cgrad[:, s, :, :] = r.gr[:, s, :, :] + r.dhs[s].astype(F32)
-    for k in (1, 2, 3):
-        homes[k - 1].wait_recv()
-        f = (s + 4 - k) % 4
-        r.cgrad[:, f, :, :] = r.gr[:, f, :, :] + r.dhr[:, f, :, :].astype(F32)
-    sd.three()
-    sa.four()
-    sd.four()
-    to_rows(sa.result(), r.fl1)
+    for h in range(4):
+        r.fl1[pl.ds(4 + h, 64, stride=4), :] = sa[h].result()
     first = sd.result()
     for k, fl in enumerate((r.fl1, r.fl2, r.fl3)):
         first_row(first[:, D * k : D * k + D], fl)
@@ -1359,8 +1425,17 @@
     squares_tail(r.sh1, r.m1, r.f1, r.s1, r.sums, d, 3 * D, 0)
     squares(r.sh2, r.m2, r.f2, r.s2, r.sums, d, 3 * D, 1, 0, 1)
     squares(r.sh3, r.m3, r.f3, r.s3, r.sums, d, 4 * D, 2, 0, 1)
+
+    def finish_input():
+        r.cgrad[:, s, :, :] = r.gr[:, s, :, :] + r.dhs[s].astype(F32)
+        for k in (1, 2, 3):
+            homes[k - 1].wait_recv()
+            f = (s + 4 - k) % 4
+            r.cgrad[:, f, :, :] = r.gr[:, f, :, :] + r.dhr[:, f, :, :].astype(F32)
+
     r.total[...], adds = sum_all(r.sums, r.ts, r.zs, r.ns, r.nq, t, s)
-    for one in (sa, sb, sc, sd):
+    finish_input()
+    for one in (*sa, sb, sc, sd):
         one.drain()
     for copy in moves + backs + moves2 + homes + adds:
         copy.wait_send()
@@ -1384,19 +1459,11 @@
     )(scnt, fcnt, cells, top, *params)
 
 
-def local(x):
-    return jnp.transpose(x.reshape(4, 32, 4, D), (0, 2, 1, 3))
-
-
-def globe(x):
-    return jnp.transpose(x, (0, 2, 1, 3)).reshape(1, 128, 4, D)
-
-
 def fast_device(cells, out_grad, scnt, fcnt, b1, f1, s1, b2, f2, s2, b3, f3, s3):
     params = (b1, f1, s1, b2, f2, s2, b3, f3, s3)
-    out, cgrad, sh1, sh2, sh3, total = call_m(scnt, fcnt, local(cells), local(out_grad), params)
-    outs = call_e(total, (sh1, sh2, sh3), params)
-    return (globe(out), globe(cgrad), *outs)
+    out, cgrad, sh1, sh2, sh3, total = call_m(scnt, fcnt, cells[0], out_grad[0], params)
+    *outs, pairs, out, cgrad = call_e(total, (sh1, sh2, sh3), params, out, cgrad)
+    return (out[None], cgrad[None], *outs, pairs.T)
 
 
 def step(*args):

time: 165 us -> 156 us (0.945)
  local copies, waits for them, and re-layouts: 7.24 us -> 0 us
    pallas_call x1, Pallas kernels: 152 us -> 148 us  [call_m(): pl.pallas_call(kernel_m, name=name, out_shape=(sds((4, 4, 32, D), BF), sd...]
    transpose x3 -> x0, local copies, waits for them, and re-layouts: 3.67 us -> none  [the longest x1 2.41 us: local(): return jnp.transpose(x.reshape(4, 32, 4, D), (0, 2, 1, 3))]
    unnamed x31 -> x0, local copies, waits for them, and re-layouts: 3.57 us -> none
    pallas_call x1, Pallas kernels: 2.93 us -> 5.95 us  [call_e(): pl.pallas_call(kernel_e, name='kernel_e', out_shape=(*shapes, sds((2, 9),...]
where the time goes in v2:
time: 156 us
  Pallas kernels  154 us (99%)
  between operations  2.13 us (1%)
    pallas_call x1, Pallas kernels, call_m(): pl.pallas_call(kernel_m, name=name, out_shape=(sds((4, 4, 32, D), BF), sd...  148 us
    pallas_call x1, Pallas kernels, call_e(): pl.pallas_call(kernel_e, name='kernel_e', out_shape=(*shapes, sds((2, 9),...  5.95 us

profile of v2, /device:TPU:0, one launch (start us, length us, event | category | flops | bytes accessed | tf_op | source)
XLA Modules:
  0.0 156.0 jit_solution(12732862478770768775)
XLA Ops:
  1.9 147.9 %kernel_m.1 = (bf16[4,4,32,512]{3,2,1,0:T(8,128)(2,1)}, f32[4,4,32,512]{3,2,1,0:T(8,128)}, f32[264,128]{1,0:T(8,128)}, f32[264,128]{1,0:T(8,128)}, f32[520,128]{1,0:T(8,128)}, /*index=5*/f32[8,128]{1,0:T(8,128)}) custom-call(s32[1]{0:T(128)S(6)} %copy.31.refs_0_, s32[1]{0:T(128)S(6)} %copy.32.refs_1_, bf16[128,4,512]{2,1,0:T(4,128)(2,1)} %bitcast.5, ...), custom_call_target="tpu_custom_call" | custom-call | tf_op jit(solution)/shard_map/kernel_m/pallas_call | solution.py:1448
  149.9 6.0 %kernel_e.1 = (f32[32784]{0:T(1024)}, f32[32784]{0:T(1024)}, f32[32784]{0:T(1024)}, f32[32784]{0:T(1024)}, bf16[32784]{0:T(1024)(128)(2,1)}, /*index=5*/f32[3278...) custom-call(f32[8,128]{1,0:T(8,128)} %get-tuple-element.42.total, ...), custom_call_target="tpu_custom_call" | custom-call | tf_op jit(solution)/shard_map/kernel_e/pallas_call | solution.py:734

commit v3 on v2

--- a/solution.py
+++ b/solution.py
@@ -684,12 +684,13 @@
     return lane == lax.broadcasted_iota(jnp.int32, (32, 128), 0)
 
 
-def sum_all(sums, ts, zs, ssem, rsem, t, s):
+def sum_all(sums, ts, zs, ssem, rsem, t, s, meanwhile):
     column = jnp.sum(sums[...], 1, keepdims=True)
     ts[t] = jnp.broadcast_to(jnp.sum(jnp.where(diagonal(32), column, 0.0), 0, keepdims=True), (8, 128))
     plane = [
         send(ts.at[t], ts.at[t], ssem.at[e - 1], rsem.at[e - 1], (jnp.bitwise_xor(t, e), s)) for e in range(1, 8)
     ]
+    meanwhile()
     for copy in plane:
         copy.wait_recv()
     zs[s] = ((ts[0] + ts[1]) + (ts[2] + ts[3])) + ((ts[4] + ts[5]) + (ts[6] + ts[7]))
@@ -797,7 +798,7 @@
     return (query % 32 == key % 32) & (key // 32 < fcnt)
 
 
-def feature_forward(qkv, o2, fcnt):
+def feature_forward(qkv, o2, fcnt, half):
     left = halves()
     one = jnp.where(left, 0.125, 0.0).astype(BF)
     two = jnp.where(left, 0.0, 0.125).astype(BF)
@@ -815,10 +816,10 @@
             o2[rows, c] = jnp.where(left, o[0:128], o[128:256]).astype(BF)
         return 0
 
-    lax.fori_loop(0, 4, body, 0)
-
-
-def feature_backward(qkv, do, dqkv, fcnt):
+    lax.fori_loop(2 * half, 2 * half + 2, body, 0)
+
+
+def feature_backward(qkv, do, dqkv, fcnt, half):
     left = halves()
     one, two = jnp.where(left, 1.0, 0.0).astype(BF), jnp.where(left, 0.0, 1.0).astype(BF)
     ok = feature_mask(fcnt, 0)
@@ -842,11 +843,17 @@
             dqkv[2, rows, c] = dv[i]
         return 0
 
-    lax.fori_loop(0, 4, body, 0)
+    lax.fori_loop(2 * half, 2 * half + 2, body, 0)
 
 
 def four_blocks(body, init=0):
     for r in range(4):
+        init = body(r, init)
+    return init
+
+
+def two_blocks(half, body, init=0):
+    for r in (2 * half, 2 * half + 1):
         init = body(r, init)
     return init
 
@@ -874,7 +881,7 @@
         wide[b, pl.ds(j, value.shape[0], stride=ways), :] = value[:, 128 * b : 128 * b + 128]
 
 
-def mlp(a3, a3t, g, h2, wup, wdn, h3, da, zb, dub, u, dz, p3):
+def mlp(a3, a3t, g, h2, wup, wdn, h3, da, zb, dub, u, dz, p3, after):
     h3[...] = h2[...]
     da[...] = jnp.zeros((512, D), F32)
 
@@ -900,14 +907,16 @@
         dw = nn(turn(zb[...]), g[...]).astype(BF)
         for i in range(4):
             p3[16 + 4 * j + i] = dw[128 * i : 128 * i + 128]
+        after(j)
         return 0
 
     lax.fori_loop(0, 4, body, 0)
 
 
-def middle_forward(s, cells, top, o1, wo1, w2, wo2, gains, scnt, fcnt, h1, h2, a2, qkv, o2, a3, g, hook):
+def middle_forward(half, s, cells, top, o1, wo1, w2, wo2, gains, scnt, fcnt, h1, h2, a2, qkv, o2, a3, g):
     gain2, gain3 = gains[1:2, :], gains[2:3, :]
-    h1[...] = nn(o1[...].reshape(512, D), wo1[...])
+    every = pl.ds(256 * half, 256)
+    h1[every, :] = nn(o1[2 * half : 2 * half + 2].reshape(256, D), wo1[...])
 
     def first(r, _):
         rows = block(r)
@@ -920,16 +929,11 @@
         g[rows, :] = jnp.where(live, flat(top[r].astype(F32)), 0.0).astype(BF)
         return 0
 
-    four_blocks(first)
-
-    def project(j, _):
-        qkv[j] = nn(a2[...], w2[j]).astype(BF)
-        return 0
-
-    lax.fori_loop(0, 3, project, 0)
-    hook()
-    feature_forward(qkv, o2, fcnt)
-    h2[...] = h1[...] + nn(o2[...], wo2[...])
+    two_blocks(half, first)
+    for j in range(3):
+        qkv[j, every, :] = nn(a2[every, :], w2[j]).astype(BF)
+    feature_forward(qkv, o2, fcnt, half)
+    h2[every, :] = h1[every, :] + nn(o2[every, :], wo2[...])
 
     def second(r, _):
         rows = block(r)
@@ -937,7 +941,7 @@
         a3[rows, :] = (x * gain3).astype(BF)
         return 0
 
-    four_blocks(second)
+    two_blocks(half, second)
 
 
 def layer_output(s, h3, lout, scnt, fcnt):
@@ -950,8 +954,9 @@
     four_blocks(last)
 
 
-def feature_grads(wo1, w2, wo2, gains, fcnt, h1, h2, qkv, g, da, b2, b1, do, dqkv, do1, gr, dgain):
+def feature_grads(half, wo1, w2, wo2, gains, fcnt, h1, h2, qkv, g, da, b2, b1, do, dqkv, do1, gr, dg2, dg3):
     gain2, gain3 = gains[1:2, :], gains[2:3, :]
+    every = pl.ds(256 * half, 256)
 
     def third(r, dg):
         rows = block(r)
@@ -961,10 +966,10 @@
         b2[rows, :] = total.astype(BF)
         return dg + part
 
-    dg3 = four_blocks(third, jnp.zeros((1, D), F32))
-    do[...] = nt(b2[...], wo2[...]).astype(BF)
-    feature_backward(qkv, do, dqkv, fcnt)
-    da[...] = nt(dqkv[0], w2[0]) + nt(dqkv[1], w2[1]) + nt(dqkv[2], w2[2])
+    dg3 = two_blocks(half, third, dg3)
+    do[every, :] = nt(b2[every, :], wo2[...]).astype(BF)
+    feature_backward(qkv, do, dqkv, fcnt, half)
+    da[every, :] = nt(dqkv[0, every, :], w2[0]) + nt(dqkv[1, every, :], w2[1]) + nt(dqkv[2, every, :], w2[2])
 
     def fourth(r, dg):
         rows = block(r)
@@ -974,10 +979,9 @@
         b1[rows, :] = total.astype(BF)
         return dg + part
 
-    dg2 = four_blocks(fourth, jnp.zeros((1, D), F32))
-    do1[...] = nt(b1[...], wo1[...]).astype(BF).reshape(4, 4, 32, D)
-    n = lax.broadcasted_iota(jnp.int32, (8, D), 0)
-    dgain[...] = jnp.where(n == 1, dg2, jnp.where(n == 2, dg3, 0.0))
+    dg2 = two_blocks(half, fourth, dg2)
+    do1[2 * half : 2 * half + 2] = nt(b1[every, :], wo1[...]).astype(BF).reshape(2, 4, 32, D)
+    return dg2, dg3
 
 
 def feature_weights(o1, a2, o2, b2, b1, dqkv, wide, p2, dwo1):
@@ -1020,12 +1024,19 @@
         t = self.t if t is None else t
         return self.part.at[pl.ds(4 * jnp.bitwise_xor(t, 2 * e), 4), *box]
 
-    def core(self):
+    def core_copy(self, e):
         tc = self.xor(1)
-        self.c = [
-            self.go(self.group(e, self.all, tc), self.r1.at[e], (tc, self.s))
-            for e in (2, 3, 1, 0)
-        ]
+        return pltpu.make_async_remote_copy(
+            src_ref=self.group(e, self.all, tc), dst_ref=self.r1.at[e], send_sem=self.ssem.at[e],
+            recv_sem=self.rsem.at[e], device_id=(tc, self.s), device_id_type=MESH,
+        )
+
+    def core(self, start=True):
+        self.c = {e: self.core_copy(e) for e in (2, 3, 1, 0)}
+        for copy in self.c.values():
+            if start:
+                copy.start()
+            self.copies.append(copy)
 
     def add(self, e, box, got):
         base = 4 * self.xor(2 * e)
@@ -1036,8 +1047,8 @@
     def one(self):
         ty, tx, s = self.xor(4), self.xor(2), self.s
         self.y, self.x = {}, {}
-        for n, e in enumerate((2, 3, 1, 0)):
-            self.c[n].wait_recv()
+        for e in (2, 3, 1, 0):
+            self.c[e].wait_recv()
             self.add(e, self.all, self.r1.at[e])
             if e in (2, 3):
                 self.y[e - 2] = self.go(self.group(e, self.ha), self.ry.at[e - 2], (ty, s))
@@ -1131,6 +1142,24 @@
 
 def top_shard(fl, d, out_ref):
     out_ref[0:8, :] = shifted(fl, d, 8)
+
+
+def early_core(red, j):
+    tc = red.xor(1)
+
+    def piece(group, rows):
+        e = jnp.bitwise_xor(tc, group) // 2
+        pltpu.make_async_remote_copy(
+            src_ref=red.part.at[pl.ds(4 * group, 4), rows], dst_ref=red.r1.at[e, :, rows], send_sem=red.ssem.at[e],
+            recv_sem=red.rsem.at[e], device_id=(tc, red.s), device_id_type=MESH,
+        ).start()
+
+    for k in (0, 2):
+        piece(jnp.bitwise_xor(tc % 4, k), pl.ds(mult(32 * j, 32), 32))
+
+    @pl.when(j % 2 == tc % 2)
+    def _():
+        piece(4 + j, pl.ds(0, 128))
 
 
 class Refs:
@@ -1182,8 +1211,8 @@
     "fl1": pltpu.VMEM((272, 128), F32), "fl2": pltpu.VMEM((272, 128), F32), "fl3": pltpu.VMEM((528, 128), F32),
     "sums": pltpu.VMEM((32, 128), F32), "ts": pltpu.VMEM((8, 8, 128), F32), "zs": pltpu.VMEM((4, 8, 128), F32),
     "gs": DMA((4, 32)), "gq": DMA((4, 32)), "rs": DMA((7, 16)), "rq": DMA((7, 16)),
-    "as1": DMA((3,)), "aq1": DMA((3,)), "as2": DMA((3,)), "aq2": DMA((3,)),
-    "as3": DMA((3,)), "aq3": DMA((3,)), "as4": DMA((3,)), "aq4": DMA((3,)), "ns": DMA((10,)), "nq": DMA((10,)),
+    "as1": DMA((3,)), "aq1": DMA((3,)), "as2": DMA((6,)), "aq2": DMA((6,)),
+    "as3": DMA((6,)), "aq3": DMA((6,)), "as4": DMA((3,)), "aq4": DMA((3,)), "ns": DMA((10,)), "nq": DMA((10,)),
 }
 INPUTS = ["scnt", "fcnt", "cells_in", "top_in"] + PARAMS
 OUTPUTS = ["lout", "cgrad", "sh1", "sh2", "sh3", "total"]
@@ -1199,13 +1228,16 @@
         Gather(buf, r.gs.at[i], r.gq.at[i], t, s) for i, buf in enumerate((r.g1, r.g2, r.g3, r.ge))
     ]
     first1 = realign(r.m1, r.sh, d, 64, r.g1, d, r.ro)
+    pl.semaphore_wait(barrier, 10)
+    ga.start_z()
+    ga.spread(0)
     first2 = realign(r.m2, r.sh, d, 64, r.g2, d, r.ro)
     first3 = realign(r.m3, r.sh, d, 128, r.g3, d, r.ro, True)
     r.ge[d] = jnp.concatenate([first1, first2, first3], 1).astype(BF).astype(F32)
-    pl.semaphore_wait(barrier, 10)
-    for one in (ge, ga, gb, gc):
-        one.start_z()
-        one.spread(0)
+    ge.start_z()
+    ge.spread(0)
+    gb.start_z()
+    gb.spread(0)
     by_feature(r.cells_in, r.cells)
     r.cf[s] = r.cells[:, s, :, :]
     for one in (ge, ga):
@@ -1214,6 +1246,8 @@
     for one in (ge, ga):
         one.near(2, 1)
         one.zin(3)
+    gc.start_z()
+    gc.spread(0)
     moves = [
         send(r.cells.at[:, (s + k) % 4], r.cf.at[s], r.as1.at[k - 1], r.aq1.at[k - 1], (t, (s + k) % 4))
         for k in (1, 2, 3)
@@ -1227,8 +1261,6 @@
         one.near(0)
         one.zin(2)
     gb.zin(1)
-    for copy in moves:
-        copy.wait_recv()
     ge.end()
     ga.end()
     gb.near(2)
@@ -1238,6 +1270,8 @@
     spread(r.g1, r.ge, 0, 64, 0, 24, put_f32(r.wide, 64))
     split_columns(r.wide, 3, r.w1)
     spread(r.g1, r.ge, 0, 64, 24, 32, put_bf(r.wo1, 64))
+    for copy in moves:
+        copy.wait_recv()
     for k in range(3):
         r.gains[k : k + 1, :] = r.ge[0, :, D * k : D * k + D]
     gain1 = r.gains[0:1, :]
@@ -1255,17 +1289,25 @@
 
     lax.fori_loop(0, 3, project, 0)
     live = lax.broadcasted_iota(jnp.int32, (1, 512), 1) < scnt
-    backs = []
     gb.near(3)
     gc.near(2)
     gc.zin(3)
+    backs = ([], [])
+
+    def give_back(k, half):
+        two = pl.ds(2 * half, 2)
+        at = 3 * half + k - 1
+        peer = (t, (s + k) % 4)
+        backs[half].append(send(r.o1c.at[k - 1, two], r.o1.at[two, s], r.as2.at[at], r.aq2.at[at], peer))
+
     for k in (2, 1, 3, 0):
-        c = (s + k) % 4
         if k:
-            attend_chunk(r.qkv1, c, live, r.o1c.at[k - 1])
-            backs.append(send(r.o1c.at[k - 1], r.o1.at[:, s], r.as2.at[k - 1], r.aq2.at[k - 1], (t, c)))
+            attend_chunk(r.qkv1, (s + k) % 4, live, r.o1c.at[k - 1])
+            give_back(k, 0)
         else:
-            attend_chunk(r.qkv1, c, live, r.o1.at[:, s])
+            for j in (2, 1, 3):
+                give_back(j, 1)
+            attend_chunk(r.qkv1, s, live, r.o1.at[:, s])
         if k == 1:
             gb.far()
             gc.near(1)
@@ -1274,12 +1316,15 @@
     split_columns(r.wide, 3, r.w2)
     spread(r.g2, r.ge, 1, 64, 24, 32, put_bf(r.wo2, 64))
     gc.near(3)
-    for copy in backs:
-        copy.wait_recv()
-    middle_forward(
-        s, r.cells, r.top, r.o1, r.wo1, r.w2, r.wo2, r.gains, scnt, fcnt, r.h1, r.h2, r.a2, r.qkv2, r.o2, r.a3, r.g,
-        gc.far,
-    )
+    for half in range(2):
+        for copy in backs[half]:
+            copy.wait_recv()
+        middle_forward(
+            half, s, r.cells, r.top, r.o1, r.wo1, r.w2, r.wo2, r.gains, scnt, fcnt, r.h1, r.h2, r.a2, r.qkv2, r.o2,
+            r.a3, r.g,
+        )
+        if half == 0:
+            gc.far()
     r.at[...] = turn(r.a3[...])
     gc.end()
 
@@ -1296,31 +1341,38 @@
     spread(r.g3, r.ge, 2, 128, 16, 32, put_down)
     for one in (ga, gb, gc, ge):
         one.drain()
-    mlp(r.a3, r.at, r.g, r.h2, r.wup, r.wdn, r.h3, r.da, r.zb, r.dub, r.u, r.dz, r.g3)
-    edge_rows(r.g3, r.ge, 2)
-
     def reducer(n, part, i, chunk=None):
         bufs = [getattr(r, k) for k in reduce_names(n)]
         return Reduce(part, *bufs, r.rs.at[i], r.rq.at[i], t, s, chunk)
 
     sb, sc, sd = reducer("b", r.g2, 0), reducer("c", r.g3, 1), reducer("d", r.ge, 2)
     sa = [reducer(f"a{h}", r.g1, 3 + h, h) for h in range(4)]
-    sc.core()
+    mlp(r.a3, r.at, r.g, r.h2, r.wup, r.wdn, r.h3, r.da, r.zb, r.dub, r.u, r.dz, r.g3, lambda j: early_core(sc, j))
+    edge_rows(r.g3, r.ge, 2)
+
+    sc.core(False)
     layer_output(s, r.h3, r.lout, scnt, fcnt)
-    feature_grads(
-        r.wo1, r.w2, r.wo2, r.gains, fcnt, r.h1, r.h2, r.qkv2, r.g, r.da, r.b, r.b1, r.do2, r.dqkv, r.do1, r.gr,
-        r.dgain,
-    )
-    moves2 = [
-        send(r.do1.at[:, (s + k) % 4], r.do.at[s], r.as3.at[k - 1], r.aq3.at[k - 1], (t, (s + k) % 4))
-        for k in (1, 2, 3)
-    ]
-    sc.one()
+    dg2 = dg3 = jnp.zeros((1, D), F32)
+    moves2 = []
+    for half in range(2):
+        if half:
+            sc.one()
+        dg2, dg3 = feature_grads(
+            half, r.wo1, r.w2, r.wo2, r.gains, fcnt, r.h1, r.h2, r.qkv2, r.g, r.da, r.b, r.b1, r.do2, r.dqkv, r.do1,
+            r.gr, dg2, dg3,
+        )
+        two = pl.ds(2 * half, 2)
+        for k in (1, 2, 3):
+            at, f = 3 * half + k - 1, (s + k) % 4
+            moves2.append(send(r.do1.at[two, f], r.do.at[s, two], r.as3.at[at], r.aq3.at[at], (t, f)))
+    n = lax.broadcasted_iota(jnp.int32, (8, D), 0)
+    r.dgain[...] = jnp.where(n == 1, dg2, jnp.where(n == 2, dg3, 0.0))
     feature_weights(r.o1, r.a2, r.o2, r.b, r.b1, r.dqkv, r.wide, r.g2, r.dwo1)
     edge_rows(r.g2, r.ge, 1)
     r.do[s] = r.do1[:, s, :, :]
     sb.core()
     r.at[...] = turn(r.a1[...])
+    sb.one()
     for copy in moves2:
         copy.wait_recv()
     live = lax.broadcasted_iota(jnp.int32, (512, 1), 0) < scnt
@@ -1347,18 +1399,18 @@
 
     heads(0)
     sc.two()
-    sb.one()
     heads(1)
     sa[0].one()
+    sb.two()
     heads(2)
-    sc.three()
     sa[1].one()
     sa[0].two()
     heads(3)
+    sc.three()
     r.da[...] = nt(r.dqkv[0], r.w1[0]) + nt(r.dqkv[1], r.w1[1]) + nt(r.dqkv[2], r.w1[2])
-    sb.two()
     sa[2].one()
     sa[1].two()
+    sb.three()
 
     def norm_back(i, dg):
         dh, part = norm_grad(r.cf[i].astype(F32).reshape(128, D), r.da[block(i), :], gain1)
@@ -1369,9 +1421,8 @@
     r.ge[0] = jnp.concatenate([dg, r.dgain[1:2, :], r.dgain[2:3, :]], 1)
     sd.core()
     sa[3].one()
+    sa[0].three()
     sc.four()
-    sb.three()
-    sa[0].three()
     sa[2].two()
     sa[1].three()
     sd.one()
@@ -1433,11 +1484,10 @@
             f = (s + 4 - k) % 4
             r.cgrad[:, f, :, :] = r.gr[:, f, :, :] + r.dhr[:, f, :, :].astype(F32)
 
-    r.total[...], adds = sum_all(r.sums, r.ts, r.zs, r.ns, r.nq, t, s)
-    finish_input()
+    r.total[...], adds = sum_all(r.sums, r.ts, r.zs, r.ns, r.nq, t, s, finish_input)
     for one in (*sa, sb, sc, sd):
         one.drain()
-    for copy in moves + backs + moves2 + homes + adds:
+    for copy in moves + backs[0] + backs[1] + moves2 + homes + adds:
         copy.wait_send()
 
 

time: 156 us -> 150 us (0.962)
  Pallas kernels: 154 us -> 147 us
    pallas_call x1, Pallas kernels: 148 us -> 141 us  [call_m(): pl.pallas_call(kernel_m, name=name, out_shape=(sds((4, 4, 32, D), BF), sd...]
where the time goes in v3:
time: 150 us
  Pallas kernels  147 us (98%)
  between operations  2.13 us (1%)
    pallas_call x1, Pallas kernels, call_m(): pl.pallas_call(kernel_m, name=name, out_shape=(sds((4, 4, 32, D), BF), sd...  141 us
    pallas_call x1, Pallas kernels, call_e(): pl.pallas_call(kernel_e, name='kernel_e', out_shape=(*shapes, sds((2, 9),...  5.95 us

profile of v3, /device:TPU:0, one launch (start us, length us, event | category | flops | bytes accessed | tf_op | source)
XLA Modules:
  0.0 149.5 jit_solution(10033811374683450661)
XLA Ops:
  1.9 141.5 %kernel_m.1 = (bf16[4,4,32,512]{3,2,1,0:T(8,128)(2,1)}, f32[4,4,32,512]{3,2,1,0:T(8,128)}, f32[264,128]{1,0:T(8,128)}, f32[264,128]{1,0:T(8,128)}, f32[520,128]{1,0:T(8,128)}, /*index=5*/f32[8,128]{1,0:T(8,128)}) custom-call(s32[1]{0:T(128)S(6)} %copy.31.refs_0_, s32[1]{0:T(128)S(6)} %copy.32.refs_1_, bf16[128,4,512]{2,1,0:T(4,128)(2,1)} %bitcast.5, ...), custom_call_target="tpu_custom_call" | custom-call | tf_op jit(solution)/shard_map/kernel_m/pallas_call | solution.py:1498
  143.4 6.0 %kernel_e.1 = (f32[32784]{0:T(1024)}, f32[32784]{0:T(1024)}, f32[32784]{0:T(1024)}, f32[32784]{0:T(1024)}, bf16[32784]{0:T(1024)(128)(2,1)}, /*index=5*/f32[3278...) custom-call(f32[8,128]{1,0:T(8,128)} %get-tuple-element.42.total, ...), custom_call_target="tpu_custom_call" | custom-call | tf_op jit(solution)/shard_map/kernel_e/pallas_call | solution.py:735

commit v4 on v3

--- a/solution.py
+++ b/solution.py
@@ -373,6 +373,15 @@
     return value if isinstance(value, int) else pl.multiple_of(value, factor)
 
 
+def repeat(lo, hi, body, ways):
+    def step(i, _):
+        for k in range(ways):
+            body(lo + i * ways + k)
+        return 0
+
+    lax.fori_loop(0, (hi - lo) // ways, step, 0)
+
+
 def nt(left, right):
     return lax.dot_general(left, right, (((1,), (1,)), ((), ())), preferred_element_type=F32)
 
@@ -515,15 +524,14 @@
 def spread(buf, firsts, kind, rows, lo, hi, put):
     tail = lax.broadcasted_iota(jnp.int32, (8, D), 0) == 7
 
-    def body(i, _):
+    def body(i):
         nxt = jnp.minimum(i + 1, 31)
         row = firsts[nxt, :, D * kind : D * kind + D]
         block = buf[i, 0:rows, :].astype(F32)
         last = block[rows - 8 : rows, :] + jnp.where(tail & (i < 31), row, 0.0)
         put(i - lo, block[0 : rows - 8, :], last)
-        return 0
-
-    lax.fori_loop(lo, hi, body, 0)
+
+    repeat(lo, hi, body, 4 if rows == 64 else 2)
 
 
 def put_f32(dst, rows):
@@ -544,14 +552,13 @@
 
 
 def split_columns(wide, ways, dst):
-    def body(i, _):
+    def body(i):
         for j in range(ways):
             for b in range(4):
                 piece = wide[b, pl.ds(64 * ways * i + j, 64, stride=ways), :]
                 dst[j, pl.ds(mult(64 * i, 64), 64), 128 * b : 128 * b + 128] = piece.astype(BF)
-        return 0
-
-    lax.fori_loop(0, 8, body, 0)
+
+    repeat(0, 8, body, 2)
 
 
 def halves():
@@ -707,39 +714,57 @@
         out[32 * g : 32 * g + 32, :, :] = jnp.transpose(x[g].astype(F32), (1, 0, 2)).astype(out.dtype)
 
 
-def kernel_e(
-    total, sh1, sh2, sh3, m1, f1, s1, m2, f2, s2, m3, f3, s3, lout, cgrad,
-    g1, fo1, so1, mo1, wo1, g2, fo2, so2, mo2, wo2, g3, fo3, so3, mo3, wo3, pairs, layer, grad,
-):
+def kernel_e(*refs):
+    ins, outs, vin, vout, sin, sout = refs[:15], refs[15:33], refs[33:48], refs[48:66], refs[66], refs[67]
     t, s = here()
     d = 4 * t + s
-    norms = jnp.sqrt(total[0:1, :])
-    pairs[0:1, :] = norms[:, 0:9]
-    pairs[1:2, :] = pltpu.roll(norms, 112, 1)[:, 0:9]
+    loads = [pltpu.make_async_copy(a, b, sin.at[i]) for i, (a, b) in enumerate(zip(ins, vin))]
+    stores = [pltpu.make_async_copy(a, b, sout.at[i]) for i, (a, b) in enumerate(zip(vout, outs))]
+    order = [0, 1, 4, 5, 6, 2, 7, 8, 9, 3, 10, 11, 12, 13, 14]
+    for i in order:
+        loads[i].start()
+    loads[0].wait()
+    norms = jnp.sqrt(vin[0][0:1, :])
+    vout[15][0:1, :] = norms[:, 0:9]
+    vout[15][1:2, :] = pltpu.roll(norms, 112, 1)[:, 0:9]
+    stores[15].start()
     norm = jnp.sum(jnp.where(diagonal(32), norms, 0.0), 1, keepdims=True)
     ratio = norm[0:9] / (norm[16:25] + 1e-6)
-    by_sample(lout, layer)
-    by_sample(cgrad, grad)
-    update(sh1, m1, f1, s1, g1, fo1, so1, mo1, wo1, ratio, d, 3 * D, 0)
-    update(sh2, m2, f2, s2, g2, fo2, so2, mo2, wo2, ratio, d, 3 * D, 1)
-    update(sh3, m3, f3, s3, g3, fo3, so3, mo3, wo3, ratio, d, 4 * D, 2)
+    for b in range(3):
+        used = [1 + b, 4 + 3 * b, 5 + 3 * b, 6 + 3 * b]
+        for i in used:
+            loads[i].wait()
+        width = 4 * D if b == 2 else 3 * D
+        update(*[vin[i] for i in used], *vout[5 * b : 5 * b + 5], ratio, d, width, b)
+        for i in range(5 * b, 5 * b + 5):
+            stores[i].start()
+    for i in (13, 14):
+        loads[i].wait()
+        by_sample(vin[i], vout[i + 3])
+        stores[i + 3].start()
+    for copy in stores:
+        copy.wait()
 
 
 def call_e(total, shards, args, lout, cgrad):
     sds = jax.ShapeDtypeStruct
-    vm = pl.BlockSpec(memory_space=pltpu.VMEM)
+    hb = pl.BlockSpec(memory_space=pl.ANY)
     shapes = []
     for m in args[0::3]:
         n = m.shape
         shapes += [sds(n, F32)] * 4 + [sds(n, BF)]
+    shapes += [sds((2, 9), F32), sds((128, 4, D), BF), sds((128, 4, D), F32)]
+    given = (total, *shards, *args, lout, cgrad)
     return pl.pallas_call(
         kernel_e,
         name="kernel_e",
-        out_shape=(*shapes, sds((2, 9), F32), sds((128, 4, D), BF), sds((128, 4, D), F32)),
-        in_specs=[vm] * 15,
-        out_specs=(vm,) * 18,
+        out_shape=tuple(shapes),
+        in_specs=[hb] * 15,
+        out_specs=(hb,) * 18,
+        scratch_shapes=[pltpu.VMEM(x.shape, x.dtype) for x in (*given, *shapes)]
+        + [pltpu.SemaphoreType.DMA((15,)), pltpu.SemaphoreType.DMA((18,))],
         compiler_params=pltpu.CompilerParams(vmem_limit_bytes=63 << 20),
-    )(total, *shards, *args, lout, cgrad)
+    )(*given)
 
 
 def backward_heads(h, qkv, do, live, dqkv, kt, dkv):
@@ -867,13 +892,12 @@
 
 
 def narrow_to(wide, part, slots, rows):
-    def body(i, _):
+    def body(i):
         at = pl.ds(mult(i * rows, rows), rows)
         for b in range(4):
             part[i, :, 128 * b : 128 * b + 128] = wide[b, at, :].astype(BF)
-        return 0
-
-    lax.fori_loop(0, slots, body, 0)
+
+    repeat(0, slots, body, 2)
 
 
 def store_wide(wide, j, ways, value):
@@ -882,25 +906,24 @@
 
 
 def mlp(a3, a3t, g, h2, wup, wdn, h3, da, zb, dub, u, dz, p3, after):
+    def act(rows):
+        x = u[rows, :]
+        cdf = 0.5 * (1.0 + lax.erf(x * 0.7071067811865476))
+        zb[rows, :] = (x * cdf).astype(BF)
+        slope = cdf + x * (0.3989422804014327 * jnp.exp(-0.5 * x * x))
+        dub[rows, :] = (slope * dz[rows, :].astype(F32)).astype(BF)
+
     h3[...] = h2[...]
     da[...] = jnp.zeros((512, D), F32)
 
     def body(j, _):
         u[...] = nn(a3[...], wup[j])
         dz[...] = nt(g[...], wdn[j]).astype(BF)
-
-        def act(r, _):
-            rows = pl.ds(mult(r * 64, 64), 64)
-            x = u[rows, :]
-            cdf = 0.5 * (1.0 + lax.erf(x * 0.7071067811865476))
-            zb[rows, :] = (x * cdf).astype(BF)
-            slope = cdf + x * (0.3989422804014327 * jnp.exp(-0.5 * x * x))
-            dub[rows, :] = (slope * dz[rows, :].astype(F32)).astype(BF)
-            return 0
-
-        lax.fori_loop(0, 8, act, 0)
-        h3[...] += nn(zb[...], wdn[j])
-        da[...] += nt(dub[...], wup[j])
+        for n in range(2):
+            rows = slice(256 * n, 256 * n + 256)
+            act(rows)
+            h3[rows, :] += nn(zb[rows, :], wdn[j])
+            da[rows, :] += nt(dub[rows, :], wup[j])
         up = nn(a3t[...], dub[...]).astype(BF)
         for i in range(16):
             p3[i, pl.ds(mult(32 * j, 32), 32), :] = up[32 * i : 32 * i + 32]
@@ -1101,12 +1124,9 @@
 def edge_rows(part, edges, kind, lo=0, size=D):
     rows = part.shape[1]
 
-    def body(i, _):
+    for i in range(1, 32):
         row = part[i - 1, rows - 16 : rows, lo : lo + size].astype(F32)[15:16, :]
         edges[i, :, D * kind + lo : D * kind + lo + size] = row
-        return 0
-
-    lax.fori_loop(1, 32, body, 0)
 
 
 def by_feature(x, out):
@@ -1195,6 +1215,11 @@
 TILE = pltpu.VMEM((4, 4, 32, D), BF)
 DMA = pltpu.SemaphoreType.DMA
 SCRATCH = {
+    "cells_in": pltpu.VMEM((128, 4, D), BF), "top_in": pltpu.VMEM((128, 4, D), BF),
+    **{k + n: pltpu.VMEM((size,), F32) for n, size in (("1", 32784), ("2", 32784), ("3", 65552)) for k in "mfs"},
+    "lout": TILE, "cgrad": pltpu.VMEM((4, 4, 32, D), F32), "sh1": pltpu.VMEM((264, 128), F32),
+    "sh2": pltpu.VMEM((264, 128), F32), "sh3": pltpu.VMEM((520, 128), F32), "total": pltpu.VMEM((8, 128), F32),
+    "ls": DMA((11,)), "os": DMA((6,)),
     "g1": pltpu.VMEM((32, 64, D), BF), "ge": pltpu.VMEM((32, 1, 3 * D), F32), "g2": pltpu.VMEM((32, 64, D), BF), "g3": pltpu.VMEM((32, 128, D), BF),
     "wide": pltpu.VMEM((4, 4 * D, 128), F32), "sh": pltpu.VMEM((536, 128), F32), "ro": pltpu.VMEM((536, 128), F32),
     "w1": THREE, "wo1": NARROW, "w2": THREE, "wo2": NARROW, "wup": FOUR, "wdn": FOUR,
@@ -1214,8 +1239,10 @@
     "as1": DMA((3,)), "aq1": DMA((3,)), "as2": DMA((6,)), "aq2": DMA((6,)),
     "as3": DMA((6,)), "aq3": DMA((6,)), "as4": DMA((3,)), "aq4": DMA((3,)), "ns": DMA((10,)), "nq": DMA((10,)),
 }
-INPUTS = ["scnt", "fcnt", "cells_in", "top_in"] + PARAMS
-OUTPUTS = ["lout", "cgrad", "sh1", "sh2", "sh3", "total"]
+LOADED = ["m1", "cells_in", "m2", "m3", "top_in", "f3", "s3", "f2", "s2", "f1", "s1"]
+INPUTS = ["scnt", "fcnt", "cells_any", "top_any"] + [k + "_any" for k in PARAMS]
+STORED = ["lout", "cgrad", "sh1", "sh2", "sh3", "total"]
+OUTPUTS = [k + "_any" for k in STORED]
 
 
 def kernel_m(*refs):
@@ -1224,6 +1251,23 @@
     d = 4 * t + s
     scnt, fcnt = r.scnt[0], r.fcnt[0]
     barrier = enter(t, s)
+    loads, stores = {}, []
+    for i, name in enumerate(LOADED):
+        source = name.replace("_in", "") + "_any"
+        loads[name] = pltpu.make_async_copy(getattr(r, source), getattr(r, name), r.ls.at[i])
+        loads[name].start()
+
+    def store(name):
+        i = STORED.index(name)
+        copy = pltpu.make_async_copy(getattr(r, name), getattr(r, name + "_any"), r.os.at[i])
+        copy.start()
+        stores.append(copy)
+
+    def params(n):
+        loads["f" + n].wait()
+        loads["s" + n].wait()
+
+    loads["m1"].wait()
     ga, gb, gc, ge = [
         Gather(buf, r.gs.at[i], r.gq.at[i], t, s) for i, buf in enumerate((r.g1, r.g2, r.g3, r.ge))
     ]
@@ -1231,6 +1275,8 @@
     pl.semaphore_wait(barrier, 10)
     ga.start_z()
     ga.spread(0)
+    loads["m2"].wait()
+    loads["m3"].wait()
     first2 = realign(r.m2, r.sh, d, 64, r.g2, d, r.ro)
     first3 = realign(r.m3, r.sh, d, 128, r.g3, d, r.ro, True)
     r.ge[d] = jnp.concatenate([first1, first2, first3], 1).astype(BF).astype(F32)
@@ -1238,6 +1284,7 @@
     ge.spread(0)
     gb.start_z()
     gb.spread(0)
+    loads["cells_in"].wait()
     by_feature(r.cells_in, r.cells)
     r.cf[s] = r.cells[:, s, :, :]
     for one in (ge, ga):
@@ -1254,6 +1301,7 @@
     ]
     for one in (ge, ga):
         one.near(3)
+    loads["top_in"].wait()
     by_feature(r.top_in, r.top)
     for one in (ge, ga):
         one.far()
@@ -1352,6 +1400,7 @@
 
     sc.core(False)
     layer_output(s, r.h3, r.lout, scnt, fcnt)
+    store("lout")
     dg2 = dg3 = jnp.zeros((1, D), F32)
     moves2 = []
     for half in range(2):
@@ -1377,11 +1426,8 @@
         copy.wait_recv()
     live = lax.broadcasted_iota(jnp.int32, (512, 1), 0) < scnt
 
-    def copy_out(i, _):
-        r.g1[24 + i] = r.dwo1[pl.ds(mult(i * 64, 64), 64), :]
-        return 0
-
-    lax.fori_loop(0, 8, copy_out, 0)
+    for i in range(8):
+        r.g1[24 + i] = r.dwo1[64 * i : 64 * i + 64, :]
 
     def heads(h):
         backward_heads(h, r.qkv1, r.do, live, r.dqkv, r.kt, r.dkv)
@@ -1389,11 +1435,10 @@
         for j in range(3):
             r.wide[h, pl.ds(j, D, stride=3), :] = nn(r.at[...], r.dqkv[j, :, cols])
 
-        def narrow(i, _):
+        def narrow(i):
             r.g1[i, :, cols] = r.wide[h, pl.ds(mult(i * 64, 64), 64), :].astype(BF)
-            return 0
-
-        lax.fori_loop(0, 24, narrow, 0)
+
+        repeat(0, 24, narrow, 4)
         edge_rows(r.g1, r.ge, 0, 128 * h, 128)
         sa[h].core()
 
@@ -1456,12 +1501,14 @@
         to_rows(main, r.fl3)
 
     to_shard(r.fl3, 128, d, r.sh3)
+    params("3")
     squares(r.sh3, r.m3, r.f3, r.s3, r.sums, d, 4 * D, 2, 1, 16)
     squares_tail(r.sh3, r.m3, r.f3, r.s3, r.sums, d, 4 * D, 2)
     sa[3].four()
     sd.four()
     to_rows(sb.result(), r.fl2)
     to_shard(r.fl2, 64, d, r.sh2)
+    params("2")
     squares(r.sh2, r.m2, r.f2, r.s2, r.sums, d, 3 * D, 1, 1, 8)
     squares_tail(r.sh2, r.m2, r.f2, r.s2, r.sums, d, 3 * D, 1)
     for h in range(4):
@@ -1472,6 +1519,9 @@
     to_shard(r.fl1, 64, d, r.sh1)
     top_shard(r.fl2, d, r.sh2)
     top_shard(r.fl3, d, r.sh3)
+    for name in ("sh1", "sh2", "sh3"):
+        store(name)
+    params("1")
     squares(r.sh1, r.m1, r.f1, r.s1, r.sums, d, 3 * D, 0, 0, 8)
     squares_tail(r.sh1, r.m1, r.f1, r.s1, r.sums, d, 3 * D, 0)
     squares(r.sh2, r.m2, r.f2, r.s2, r.sums, d, 3 * D, 1, 0, 1)
@@ -1483,17 +1533,21 @@
             homes[k - 1].wait_recv()
             f = (s + 4 - k) % 4
             r.cgrad[:, f, :, :] = r.gr[:, f, :, :] + r.dhr[:, f, :, :].astype(F32)
+        store("cgrad")
 
     r.total[...], adds = sum_all(r.sums, r.ts, r.zs, r.ns, r.nq, t, s, finish_input)
+    store("total")
     for one in (*sa, sb, sc, sd):
         one.drain()
     for copy in moves + backs[0] + backs[1] + moves2 + homes + adds:
         copy.wait_send()
+    for copy in stores:
+        copy.wait()
 
 
 def call_m(scnt, fcnt, cells, top, params, name="kernel_m"):
     sds = jax.ShapeDtypeStruct
-    vm = pl.BlockSpec(memory_space=pltpu.VMEM)
+    hb = pl.BlockSpec(memory_space=pl.ANY)
     sm = pl.BlockSpec(memory_space=pltpu.SMEM)
     return pl.pallas_call(
         kernel_m,
@@ -1502,8 +1556,8 @@
             sds((4, 4, 32, D), BF), sds((4, 4, 32, D), F32), sds((264, 128), F32), sds((264, 128), F32),
             sds((520, 128), F32), sds((8, 128), F32),
         ),
-        in_specs=[sm, sm] + [vm] * 11,
-        out_specs=(vm,) * 6,
+        in_specs=[sm, sm] + [hb] * 11,
+        out_specs=(hb,) * 6,
         scratch_shapes=list(SCRATCH.values()),
         compiler_params=pltpu.CompilerParams(collective_id=1, has_side_effects=True, vmem_limit_bytes=63 << 20),
     )(scnt, fcnt, cells, top, *params)

time: 150 us -> 142 us (0.947)
  Pallas kernels: 147 us -> 140 us
    pallas_call x1, Pallas kernels: 141 us -> 136 us  [call_m(): pl.pallas_call(kernel_m, name=name, out_shape=(sds((4, 4, 32, D), BF), sd...]
    pallas_call x1, Pallas kernels: 5.95 us -> 4.33 us  [call_e(): pl.pallas_call(kernel_e, name='kernel_e', out_shape=tuple(shapes), in_spe...]
where the time goes in v4:
time: 142 us
  Pallas kernels  140 us (99%)
  between operations  2.14 us (2%)
    pallas_call x1, Pallas kernels, call_m(): pl.pallas_call(kernel_m, name=name, out_shape=(sds((4, 4, 32, D), BF), sd...  136 us
    pallas_call x1, Pallas kernels, call_e(): pl.pallas_call(kernel_e, name='kernel_e', out_shape=tuple(shapes), in_spe...  4.33 us

profile of v4, /device:TPU:0, one launch (start us, length us, event | category | flops | bytes accessed | tf_op | source)
XLA Modules:
  0.0 142.3 jit_solution(17081031630544762918)
XLA Ops:
  1.9 135.8 %kernel_m.1 = (bf16[4,4,32,512]{3,2,1,0:T(8,128)(2,1)}, f32[4,4,32,512]{3,2,1,0:T(8,128)}, f32[264,128]{1,0:T(8,128)}, f32[264,128]{1,0:T(8,128)}, f32[520,128]{1,0:T(8,128)}, /*index=5*/f32[8,128]{1,0:T(8,128)}) custom-call(s32[1]{0:T(128)S(6)} %copy.31.refs_0_, s32[1]{0:T(128)S(6)} %copy.32.refs_1_, bf16[128,4,512]{2,1,0:T(4,128)(2,1)} %bitcast.5, ...), custom_call_target="tpu_custom_call" | custom-call | tf_op jit(solution)/shard_map/kernel_m/pallas_call | solution.py:1552
  137.7 4.3 %kernel_e.1 = (f32[32784]{0:T(1024)}, f32[32784]{0:T(1024)}, f32[32784]{0:T(1024)}, f32[32784]{0:T(1024)}, bf16[32784]{0:T(1024)(128)(2,1)}, /*index=5*/f32[3278...) custom-call(f32[8,128]{1,0:T(8,128)} %get-tuple-element.42.refs_0_, ...), custom_call_target="tpu_custom_call" | custom-call | tf_op jit(solution)/shard_map/kernel_e/pallas_call | solution.py:758

commit v5 on v4

--- a/solution.py
+++ b/solution.py
@@ -610,9 +610,9 @@
     return fn, sn, fn / (jnp.sqrt(sn) + 1e-6)
 
 
-def flat_index():
-    rows = lax.broadcasted_iota(jnp.int32, (32, 128), 0)
-    return rows * 128 + lax.broadcasted_iota(jnp.int32, (32, 128), 1)
+def flat_index(rows=32):
+    lane = lax.broadcasted_iota(jnp.int32, (rows, 128), 1)
+    return lax.broadcasted_iota(jnp.int32, (rows, 128), 0) * 128 + lane
 
 
 def fold(x):
@@ -659,7 +659,7 @@
 
 def update(sh, m, f, s, grad, fout, sout, mout, wout, ratio, d, width, b):
     entries = m.shape[0]
-    whole = entries // 4096
+    whole = entries // 8192
     ends = edges(d, entries, width)
     half = [0.5 * ratio[3 * b + k : 3 * b + k + 1, :] for k in range(3)]
 
@@ -674,16 +674,16 @@
         mout[at] = new
         wout[at] = new.astype(BF)
 
-    index = flat_index()
+    index = flat_index(64)
 
     def body(i, _):
-        at = pl.ds(mult(i * 4096, 4096), 4096)
-        put(at, sh[pl.ds(mult(i * 32, 32), 32), :], segment(index + i * 4096, ends), (32, 128))
+        at = pl.ds(mult(i * 8192, 8192), 8192)
+        put(at, sh[pl.ds(mult(i * 64, 64), 64), :], segment(index + i * 8192, ends), (64, 128))
         return 0
 
     lax.fori_loop(0, whole, body, 0)
-    part = segment(lax.broadcasted_iota(jnp.int32, (1, 16), 1) + whole * 4096, ends)
-    put(pl.ds(whole * 4096, 16), sh[32 * whole : 32 * whole + 1, 0:16], part, (1, 16))
+    part = segment(lax.broadcasted_iota(jnp.int32, (1, 16), 1) + whole * 8192, ends)
+    put(pl.ds(whole * 8192, 16), sh[64 * whole : 64 * whole + 1, 0:16], part, (1, 16))
 
 
 def diagonal(rows):

time: 142 us -> 142 us (level)
  no operation moved by 1% of the time
where the time goes in v5:
time: 142 us
  Pallas kernels  140 us (99%)
  between operations  2.14 us (2%)
    pallas_call x1, Pallas kernels, call_m(): pl.pallas_call(kernel_m, name=name, out_shape=(sds((4, 4, 32, D), BF), sd...  136 us
    pallas_call x1, Pallas kernels, call_e(): pl.pallas_call(kernel_e, name='kernel_e', out_shape=tuple(shapes), in_spe...  3.98 us

profile of v5, /device:TPU:0, one launch (start us, length us, event | category | flops | bytes accessed | tf_op | source)
XLA Modules:
  0.0 141.9 jit_solution(9739361334643292390)
XLA Ops:
  1.9 135.8 %kernel_m.1 = (bf16[4,4,32,512]{3,2,1,0:T(8,128)(2,1)}, f32[4,4,32,512]{3,2,1,0:T(8,128)}, f32[264,128]{1,0:T(8,128)}, f32[264,128]{1,0:T(8,128)}, f32[520,128]{1,0:T(8,128)}, /*index=5*/f32[8,128]{1,0:T(8,128)}) custom-call(s32[1]{0:T(128)S(6)} %copy.31.refs_0_, s32[1]{0:T(128)S(6)} %copy.32.refs_1_, bf16[128,4,512]{2,1,0:T(4,128)(2,1)} %bitcast.5, ...), custom_call_target="tpu_custom_call" | custom-call | tf_op jit(solution)/shard_map/kernel_m/pallas_call | solution.py:1552
  137.7 4.0 %kernel_e.1 = (f32[32784]{0:T(1024)}, f32[32784]{0:T(1024)}, f32[32784]{0:T(1024)}, f32[32784]{0:T(1024)}, bf16[32784]{0:T(1024)(128)(2,1)}, /*index=5*/f32[3278...) custom-call(f32[8,128]{1,0:T(8,128)} %get-tuple-element.42.refs_0_, ...), custom_call_target="tpu_custom_call" | custom-call | tf_op jit(solution)/shard_map/kernel_e/pallas_call | solution.py:758
